TPU v7x, 1024 devices: a whole 8x8x8 slice. The times are simulated.
1024 devices in a mesh: wave: 64 (over y_lo, x, core), lev: 16 (over y_hi, z).
Axes of the slice: x: 8, y: 8 (y_hi: 2, y_lo: 4; y = y_hi * 4 + y_lo), z: 8, core: 2. Of those that a mesh axis runs over, the one named last changes fastest.
Arguments:
- vort_div: float32 [4, 16, 640, 640], P(None, 'lev', 'wave'), may hold values from -0.4 to 0.4
- legendre: float32 [640, 64, 640], P('wave'), may hold values from -0.3125 to 0.3125
- owner_map: int32 [640], replicated, may hold values from 0 to 639, as said below
- lat_sine: float32 [64], P('wave'), may hold values from -0.9 to 0.9
- quad_weight: float32 [64], P('wave'), may hold values from 2 to 6
- thickness: float32 [16], P('lev'), may hold values from 0.02 to 0.08
- tracers: float32 [8, 16, 64, 1280], P(None, 'lev', 'wave'), may hold values from -6 to 6
Outputs:
- tendency: float32 [8, 2, 16, 640, 640], P(None, None, 'lev', 'wave')
Inputs may be any that keep to these rules, and one draw needn't show every extreme that they name: `owner_map`: a permutation of the 640 wavenumbers in which slots 2 i and 2 i + 1 hold m and 639 - m.
All inputs are finite; a program needn't handle non-finite values.
Results may differ from a plain program's by a relative error of at most 0.00007.
Values sent between devices are 32-bit elements; how exact they have to be, the bound alone decides.
No kernel may reach another device: no remote copies, remote signals or barrier semaphores. Data moves between devices by JAX's collectives and lax.ppermute only.
A program may use at most 32 MiB of HBM per device.

v0:
```python
import math

import jax
import jax.numpy as jnp
from jax import lax
from jax.experimental import pallas as pl
from jax.experimental.pallas import tpu as pltpu
from jax.sharding import PartitionSpec as P

planet_radius = 20.0
INTERPRET = False
f32 = jnp.float32
bf16 = jnp.bfloat16

vmem = pl.BlockSpec(memory_space=pltpu.VMEM)
smem = pl.BlockSpec(memory_space=pltpu.SMEM)


def halves(x):
    high = x.astype(bf16)
    low = (x - high.astype(f32)).astype(bf16)
    return high, low


def dot_nn(left, right):
    return lax.dot_general(left, right, (((1,), (0,)), ((), ())), preferred_element_type=f32)


def dot_nt(left, right):
    return lax.dot_general(left, right, (((1,), (1,)), ((), ())), preferred_element_type=f32)


def three_products(left, right_high, right_low, dot):
    rows = left.shape[0]
    high, low = halves(left)
    both = dot(jnp.concatenate([high, low], axis=0), right_high)
    return both[:rows] + both[rows:] + dot(high, right_low)


def cos_sin(steps, quarter):
    turns = jnp.floor(steps * (1.0 / quarter) + 0.5)
    angle = (steps - turns * quarter) * (0.5 * math.pi / quarter)
    z = angle * angle
    sine = ((-1.9515295891e-4 * z + 8.3321608736e-3) * z - 1.6666654611e-1) * z * angle + angle
    cosine = (
        (2.443315711809948e-5 * z - 1.388731625493765e-3) * z + 4.166664568298827e-2
    ) * z * z - 0.5 * z + 1.0
    turn = turns.astype(jnp.int32)
    odd = (turn & 1) == 1
    first = jnp.where(odd, sine, cosine)
    second = jnp.where(odd, cosine, sine)
    return (
        jnp.where(((turn + 1) & 2) == 2, -first, first),
        jnp.where((turn & 2) == 2, -second, second),
    )


def winds_kernel(vort_ref, leg_ref, order_ref, thick_ref, f_ref, lev_ref, ft_ref, msg_ref):
    slots, rows, degrees = leg_ref.shape
    copies = lev_ref.shape[0] // slots
    tiles = degrees // 128
    order = order_ref[...].astype(f32)

    def vort(part):
        start = part * slots * tiles
        return jnp.concatenate(
            [vort_ref[pl.ds(start + tile, slots, stride=tiles), :] for tile in range(tiles)], axis=1
        )

    degree = lax.broadcasted_iota(jnp.int32, (slots, degrees), 1).astype(f32)

    def coupling_at(n):
        ratio = jnp.maximum(n * n - order * order, 0.0) / jnp.maximum(4.0 * n * n - 1.0, 1.0)
        return jnp.where(n > order, jnp.sqrt(ratio), 0.0)

    coupling = coupling_at(degree)
    last = degree == degrees - 1
    coupling_next = jnp.where(last, 0.0, coupling_at(degree + 1.0))
    lower_factor = -(degree - 1.0) * coupling
    upper_factor = (degree + 2.0) * coupling_next
    inverse = jnp.where(
        degree > 0, -planet_radius * planet_radius / jnp.maximum(degree * (degree + 1.0), 1.0), 0.0
    )
    valid = degree >= order

    def derivative(field):
        lower = jnp.where(degree == 0, 0.0, pltpu.roll(field, 1, 1))
        upper = jnp.where(last, 0.0, pltpu.roll(field, degrees - 1, 1))
        return lower_factor * lower + upper_factor * upper

    div_real = vort(2)
    div_imag = vort(3)
    stream_real = inverse * vort(0)
    stream_imag = inverse * vort(1)
    potential_real = inverse * div_real
    potential_imag = inverse * div_imag
    scale = 1.0 / planet_radius
    thickness = thick_ref[0]
    zeros = jnp.zeros((slots, degrees), f32)
    fields = [
        (-order * potential_imag - derivative(stream_real)) * scale,
        (-order * stream_imag + derivative(potential_real)) * scale,
        div_real * thickness,
        zeros,
        (order * potential_real - derivative(stream_imag)) * scale,
        (order * stream_real + derivative(potential_imag)) * scale,
        div_imag * thickness,
        zeros,
    ]
    fields = [jnp.where(valid, field, 0.0) for field in fields]
    total = jnp.zeros((rows, 128), f32)
    for s in range(slots):
        lane = (s % 2) * 64 + (s // 2) * 8
        block = jnp.concatenate([field[s : s + 1] for field in fields], axis=0)
        parts = [block]
        if lane > 0:
            parts.insert(0, jnp.zeros((lane, degrees), f32))
        if lane + 8 < 128:
            parts.append(jnp.zeros((128 - lane - 8, degrees), f32))
        block_high, block_low = halves(jnp.concatenate(parts, axis=0))
        total = total + three_products(leg_ref[s], block_high, block_low, dot_nt)
    f_ref[...] = total
    ft_ref[...] = total.T
    for s in range(slots):
        lane = (s % 2) * 64 + (s // 2) * 8
        msg_ref[s : s + 1, 0:rows] = ft_ref[lane + 2 : lane + 3, :]
        msg_ref[s : s + 1, rows : 2 * rows] = ft_ref[lane + 6 : lane + 7, :]
    message = msg_ref[...]
    for copy in range(copies):
        lev_ref[copy * slots : (copy + 1) * slots, :] = message


def table_kernel(owner_ref, table_high_ref, table_low_ref, phase_cos_ref, phase_sin_ref):
    waves, slots = owner_ref.shape
    length = 2.0 * waves * slots
    orders = owner_ref[...].astype(f32)
    offset = lax.broadcasted_iota(jnp.int32, (waves, 128), 1).astype(f32)
    padded = jnp.concatenate([orders, jnp.zeros((waves, 128 - slots), f32)], axis=1)
    by_slot = padded.T
    blocks = phase_cos_ref.shape[0] // (slots // 2)
    block = lax.broadcasted_iota(jnp.int32, (blocks, 128), 0).astype(f32)
    for s in range(slots):
        cosine, sine = cos_sin(orders[:, s : s + 1] * offset, length / 4.0)
        cos_high, cos_low = halves(cosine)
        sin_high, sin_low = halves(-sine)
        rows = slice(s * waves, (s + 1) * waves)
        table_high_ref[rows, 0:128] = cos_high
        table_high_ref[rows, 128:256] = sin_high
        table_low_ref[rows, 0:128] = cos_low
        table_low_ref[rows, 128:256] = sin_low
    for t in range(slots // 2):
        row = jnp.concatenate([by_slot[2 * t : 2 * t + 1, :], by_slot[2 * t + 1 : 2 * t + 2, :]], axis=1)
        cosine, sine = cos_sin(row * block * 128.0, length / 4.0)
        phase_cos_ref[t * blocks : (t + 1) * blocks, :] = cosine
        phase_sin_ref[t * blocks : (t + 1) * blocks, :] = sine


def prefix_kernel(got_ref, f_ref, level_ref, out_ref, ft_ref):
    rows = f_ref.shape[0]
    slots = 10
    copies = got_ref.shape[0] // slots
    level = level_ref[0]
    total = jnp.zeros((slots, 128), f32)
    for source in range(copies):
        total = total + jnp.where(source < level, got_ref[source * slots : (source + 1) * slots, :], 0.0)
    ft_ref[...] = jnp.zeros((128, rows), f32)
    for s in range(slots):
        lane = (s % 2) * 64 + (s // 2) * 8
        ft_ref[lane + 3 : lane + 4, :] = total[s : s + 1, 0:rows]
        ft_ref[lane + 7 : lane + 8, :] = total[s : s + 1, rows : 2 * rows]
    out_ref[...] = f_ref[...] + ft_ref[...].T


def grid_kernel(
    got_ref,
    table_high_ref,
    table_low_ref,
    phase_cos_ref,
    phase_sin_ref,
    q_ref,
    above_ref,
    below_ref,
    sine_ref,
    weight_ref,
    thick_ref,
    out_ref,
):
    waves = got_ref.shape[0]
    pairs = 5
    blocks = phase_cos_ref.shape[0] // pairs
    used = q_ref.shape[0] // 8
    got = got_ref[...]
    stacked = jnp.concatenate([got, pltpu.roll(got, 64, 1)], axis=0).T
    sign = jnp.where(lax.broadcasted_iota(jnp.int32, (8, 128), 0) < 4, -1.0, 1.0)
    plain = [stacked[8 * t : 8 * t + 8] for t in range(pairs)]
    swapped = [pltpu.roll(x, 4, 0) * sign for x in plain]
    phase_cos = [[phase_cos_ref[t * blocks + b : t * blocks + b + 1, :] for t in range(pairs)] for b in range(used)]
    phase_sin = [[phase_sin_ref[t * blocks + b : t * blocks + b + 1, :] for t in range(pairs)] for b in range(used)]
    turned = jnp.concatenate(
        [
            jnp.concatenate(
                [plain[t] * phase_cos[b][t] + swapped[t] * phase_sin[b][t] for t in range(pairs)], axis=1
            )
            for b in range(used)
        ],
        axis=0,
    )
    table_high = table_high_ref[...]
    table_low = table_low_ref[...]
    grid = three_products(turned, table_high, table_low, dot_nn)
    length = 128.0 * used
    lon_step = 2.0 * math.pi / length
    lat_step = 2.0 * math.pi / length
    sine = sine_ref[0]
    metric = 1.0 - sine * sine
    weight = -weight_ref[0] * (2.0 / length)
    zonal_factor = weight / (metric * (2.0 * lon_step))
    merid_factor = weight / (metric * (2.0 * lat_step))
    vertical_factor = weight / (2.0 * thick_ref[0])
    lane = lax.broadcasted_iota(jnp.int32, (8, 128), 1)
    tracer, east, other, merid = [], [], [], []
    for b in range(used):
        q = q_ref[pl.ds(b, 8, stride=used), :]
        above = above_ref[pl.ds(b, 8, stride=used), :]
        below = below_ref[pl.ds(b, 8, stride=used), :]
        field = grid[8 * b : 8 * b + 4, 0:128] + grid[8 * b + 4 : 8 * b + 8, 128:256]
        east.append(field[0:1] * q)
        merid.append(field[1:2] * q)
        other.append((field[3:4] * (above - below) - field[2:3] * (q + below)) * vertical_factor)
    ahead = [pltpu.roll(z, 127, 1) for z in east]
    behind = [pltpu.roll(z, 1, 1) for z in east]
    rest = []
    for b in range(used):
        right = jnp.where(lane == 127, ahead[(b + 1) % used], ahead[b])
        left = jnp.where(lane == 0, behind[(b - 1) % used], behind[b])
        rest.append(other[b] + zonal_factor * (right - left))
    values = jnp.concatenate(rest + merid, axis=0)
    along_cos = three_products(values, table_high[:, 0:128], table_low[:, 0:128], dot_nt)
    along_sin = three_products(values, table_high[:, 128:256], table_low[:, 128:256], dot_nt)
    for kind in range(2):
        stack = []
        for t in range(pairs):
            cos_total = jnp.zeros((8, 128), f32)
            sin_total = jnp.zeros((8, 128), f32)
            for b in range(used):
                row = 8 * (kind * used + b)
                c = along_cos[row : row + 8, 128 * t : 128 * t + 128]
                s = along_sin[row : row + 8, 128 * t : 128 * t + 128]
                cos_total = cos_total + phase_cos[b][t] * c + phase_sin[b][t] * s
                sin_total = sin_total + phase_cos[b][t] * s - phase_sin[b][t] * c
            stack += [cos_total, sin_total]
        stack.append(jnp.full((128 - 16 * pairs, 128), merid_factor, f32))
        sent = jnp.concatenate(stack, axis=0).T
        for parity in range(2):
            out_ref[pl.ds(kind * 2 + parity, waves, stride=4), :] = sent[parity * 64 : parity * 64 + waves]


def result_kernel(got_ref, leg_ref, order_ref, out_ref):
    slots, rows, degrees = leg_ref.shape
    tiles = degrees // 128
    zero_row = jnp.zeros((1, 128), f32)
    parts = []
    for parity in range(2):
        rest = got_ref[pl.ds(parity, rows, stride=4), :]
        merid = got_ref[pl.ds(2 + parity, rows, stride=4), :]
        factor = rest[:, 80:81]
        north = jnp.concatenate([merid[1:], zero_row], axis=0)
        south = jnp.concatenate([zero_row, merid[:-1]], axis=0)
        parts.append(rest + factor * (north - south))
    stacked = jnp.concatenate(parts, axis=0).T
    first = lax.broadcasted_iota(jnp.int32, (16, 2 * rows), 1) < rows
    degree = lax.broadcasted_iota(jnp.int32, (8, degrees), 1)
    for t in range(slots // 2):
        block = stacked[16 * t : 16 * t + 16]
        left = jnp.concatenate([jnp.where(first, block, 0.0), jnp.where(first, 0.0, block)], axis=0)
        right = leg_ref[2 * t : 2 * t + 2].reshape(2 * rows, degrees)
        right_high, right_low = halves(right)
        product = three_products(left, right_high, right_low, dot_nn)
        for parity in range(2):
            s = 2 * t + parity
            valid = degree >= order_ref[s]
            for part in range(2):
                row = parity * 16 + part * 8
                kept = jnp.where(valid, product[row : row + 8], 0.0)
                for tile in range(tiles):
                    start = (part * slots + s) * tiles + tile
                    out_ref[pl.ds(start, 8, stride=2 * slots * tiles), :] = kept[:, 128 * tile : 128 * tile + 128]


def local(x):
    return x if INTERPRET else pltpu.with_memory_space_constraint(x, pltpu.VMEM)


def shaped(shape, dtype=f32):
    return jax.ShapeDtypeStruct(shape, dtype) if INTERPRET else pltpu.VMEM(shape, dtype)


def shards(vort_div, legendre, owner_map, lat_sine, quad_weight, thickness, tracers):
    slots, rows, degrees = legendre.shape
    waves = lax.axis_size("wave")
    levels = lax.axis_size("lev")
    count, _, _, length = tracers.shape
    call = lambda kernel, **kw: pl.pallas_call(kernel, interpret=INTERPRET, **kw)
    up = [(i, i + 1) for i in range(levels - 1)]
    down = [(b, a) for a, b in up]
    above = lax.ppermute(tracers, "lev", up)
    below = lax.ppermute(tracers, "lev", down)
    legendre = local(legendre)
    own = lax.dynamic_slice_in_dim(owner_map, lax.axis_index("wave") * slots, slots)
    level = lax.axis_index("lev").astype(jnp.int32).reshape(1)
    fourier, message = call(
        winds_kernel,
        name="winds",
        in_specs=[vmem, vmem, vmem, smem],
        out_specs=(vmem, vmem),
        out_shape=(
            shaped((rows, 128)),
            shaped((levels * slots, 128)),
        ),
        scratch_shapes=[pltpu.VMEM((128, rows), f32), pltpu.VMEM((slots, 128), f32)],
    )(local(vort_div.reshape(4 * slots * degrees // 128, 128)), legendre, local(own.reshape(slots, 1)), thickness)
    totals = lax.all_to_all(
        message.reshape(levels, 1, slots * 128), "lev", split_axis=0, concat_axis=0, tiled=True
    ).reshape(levels * slots, 128)
    table_high, table_low, phase_cos, phase_sin = call(
        table_kernel,
        name="tables",
        in_specs=[vmem],
        out_specs=(vmem, vmem, vmem, vmem),
        out_shape=(
            shaped((waves * slots, 256), bf16),
            shaped((waves * slots, 256), bf16),
            shaped((slots // 2 * 16, 128)),
            shaped((slots // 2 * 16, 128)),
        ),
    )(local(owner_map.reshape(waves, slots)))
    sent = call(
        prefix_kernel,
        name="prefix",
        in_specs=[vmem, vmem, smem],
        out_specs=vmem,
        out_shape=shaped((rows, 128)),
        scratch_shapes=[pltpu.VMEM((128, rows), f32)],
    )(local(totals), local(fourier), level)
    got = lax.all_to_all(
        sent.reshape(rows, 1, 128), "wave", split_axis=0, concat_axis=0, tiled=True
    ).reshape(waves, 128)
    flat = lambda x: local(x.reshape(count * length // 128, 128))
    spectra = call(
        grid_kernel,
        name="grid",
        in_specs=[vmem] * 8 + [smem] * 3,
        out_specs=vmem,
        out_shape=shaped((waves * 4, 128)),
    )(
        local(got),
        local(table_high),
        local(table_low),
        local(phase_cos),
        local(phase_sin),
        flat(tracers),
        flat(above),
        flat(below),
        lat_sine,
        quad_weight,
        thickness,
    )
    back = lax.all_to_all(
        spectra.reshape(waves, 4, 128), "wave", split_axis=0, concat_axis=0, tiled=True
    ).reshape(rows * 4, 128)
    result = call(
        result_kernel,
        name="result",
        in_specs=[vmem, vmem, smem],
        out_specs=vmem,
        out_shape=jax.ShapeDtypeStruct((count * 2 * slots * degrees // 128, 128), f32),
    )(local(back), legendre, own)
    return result.reshape(count, 2, 1, slots, degrees)


def solution(mesh):
    placed = (
        P(None, "lev", "wave", None),
        P("wave", None, None),
        P(),
        P("wave"),
        P("wave"),
        P("lev"),
        P(None, "lev", "wave", None),
    )
    return jax.shard_map(
        shards,
        mesh=mesh,
        in_specs=placed,
        out_specs=P(None, None, "lev", "wave", None),
        check_vma=False,
    )
```

profile of v0, /device:TPU:113, one launch (start us, length us, event | category | flops | bytes accessed | tf_op | source)
XLA Modules:
  0.0 90.2 jit_solution(17436909521015301422)
XLA Ops:
  0.0 0.0 copy-start.4
  0.7 0.8 dynamic-slice_bitcast_fusion
  1.4 0.1 copy.12.order_ref
  1.5 0.0 copy-start
  1.5 1.4 %copy-done = f32[10,64,640]{2,1,0:T(8,128)S(1)} copy-done((f32[10,64,640]{2,1,0:T(8,128)S(1)}, f32[10,64,640]{2,1,0:T(8,128)}, u32[]{:S(2)}) %copy-start) | copy-done | bytes 1638424
  3.0 0.0 copy-start.2
  3.0 0.9 copy-done.2
  3.9 0.0 copy-start.3
  3.9 0.0 copy-start.1
  3.9 2.1 %winds.1 = (f32[64,128]{1,0:T(8,128)S(1)}, f32[160,128]{1,0:T(8,128)}) custom-call(f32[200,128]{1,0:T(8,128)S(1)} %bitcast.19, f32[10,64,640]{2,1,0:T(8,128)S(1)} %copy-done, s32[10,1]{1,0:T(8,128)S(1)} %copy.12.order_ref, f32[1]{0:T(128)S(6)} %copy.18.thick_ref), custom_call_target="tpu_custom_call" | custom-call | tf_op jit(solution)/shard_map/winds/pallas_call | solution.py:311
  6.0 21.5 %all-to-all-start = ((f32[16,1,1280]{2,1,0:T(1,128)}), f32[16,1,1280]{2,1,0:T(1,128)S(1)}, u32[]{:S(2)}, u32[]{:S(2)}) async-start(f32[16,1,1280]{2,1,0:T(1,128)} %bitcast.2), calls=%async_computation | async-start | bytes 163840 | tf_op jit(solution)/shard_map/all_to_all | solution.py:322
  27.5 6.9 %all-to-all-done = f32[16,1,1280]{2,1,0:T(1,128)S(1)} async-done(((f32[16,1,1280]{2,1,0:T(1,128)}), f32[16,1,1280]{2,1,0:T(1,128)S(1)}, u32[]{:S(2)}, u32[]{:S(2)}) %all-to-all-start) | async-done | bytes 81952 | tf_op jit(solution)/shard_map/all_to_all | solution.py:322
  34.4 0.8 prefix.1
  35.2 12.0 %all-to-all-start.1 = ((f32[64,1,128]{2,1,0:T(1,128)}), f32[64,1,128]{2,1,0:T(1,128)S(1)}, u32[]{:S(2)}, u32[]{:S(2)}) async-start(f32[64,1,128]{2,1,0:T(1,128)} %bitcast.6), calls=%async_computation.1 | async-start | bytes 65536 | tf_op jit(solution)/shard_map/all_to_all | solution.py:345
  47.2 0.0 copy-done.3
  47.2 7.4 %collective-permute-start.1 = (f32[8,1,1,1280]{3,2,1,0:T(1,128)S(1)}, f32[8,1,1,1280]{3,2,1,0:T(1,128)S(1)}, u32[]{:S(2)}, u32[]{:S(2)}) collective-permute-start(f32[8,1,1,1280]{3,2,1,0:T(1,128)S(1)} %copy-done.3), channel_id=1, source_target_pairs={{1,0},{2,1},{3,2},{4,3},{5,4},{6,5},{7,6},{8,7},{9,8},{10,9},{11,1... | collective-permute-start | bytes 122888 | tf_op jit(solution)/shard_map/ppermute | solution.py:307
  54.7 1.9 %collective-permute-start = (f32[8,1,1,1280]{3,2,1,0:T(1,128)S(1)}, f32[8,1,1,1280]{3,2,1,0:T(1,128)S(1)}, u32[]{:S(2)}, u32[]{:S(2)}) collective-permute-start(f32[8,1,1,1280]{3,2,1,0:T(1,128)S(1)} %copy-done.3), channel_id=1, source_target_pairs={{0,1},{1,2},{2,3},{3,4},{4,5},{5,6},{6,7},{7,8},{8,9},{9,10},{10,1... | collective-permute-start | bytes 122888 | tf_op jit(solution)/shard_map/ppermute | solution.py:306
  56.6 0.0 copy-done.4
  56.6 0.1 reshape.49.owner_ref
  58.0 0.7 tables.1
  58.7 0.0 collective-permute-done.1
  58.7 6.7 %collective-permute-done = f32[8,1,1,1280]{3,2,1,0:T(1,128)S(1)} collective-permute-done((f32[8,1,1,1280]{3,2,1,0:T(1,128)S(1)}, f32[8,1,1,1280]{3,2,1,0:T(1,128)S(1)}, u32[]{:S(2)}, u32[]{:S(2)}) %collective-permute-start) | collective-permute-done | bytes 40992 | tf_op jit(solution)/shard_map/ppermute | solution.py:306
  65.4 0.0 all-to-all-done.1
  65.4 1.8 %grid.1 = f32[256,128]{1,0:T(8,128)} custom-call(f32[64,128]{1,0:T(8,128)S(1)} %bitcast.18, bf16[640,256]{1,0:T(8,128)(2,1)S(1)} %get-tuple-element.13.table_high_ref, bf16[640,256]{1,0:T(8,128)(2,1)S(1)} %get-tuple-element.14.table_low_ref, f32[80,128]{1,0:T(8,128)S(1)} %get-tuple-element.15.phase_cos_ref, f32[80,128]{1,0:T(8,128)S(1)} %get-tuple-element.16.phase_sin_ref, ...), custom_call_target="tpu_custom_call" | custom-call | tf_op jit(solution)/shard_map/grid/pallas_call | solution.py:349
  67.2 12.2 %all-to-all-start.2 = ((f32[64,4,128]{2,1,0:T(4,128)}), f32[64,4,128]{2,1,0:T(4,128)S(1)}, u32[]{:S(2)}, u32[]{:S(2)}) async-start(f32[64,4,128]{2,1,0:T(4,128)} %bitcast.11), calls=%async_computation.2 | async-start | bytes 262144 | tf_op jit(solution)/shard_map/all_to_all | solution.py:368
  79.4 0.6 dynamic_slice.3.order_ref
  80.0 8.2 %all-to-all-done.2 = f32[64,4,128]{2,1,0:T(4,128)S(1)} async-done(((f32[64,4,128]{2,1,0:T(4,128)}), f32[64,4,128]{2,1,0:T(4,128)S(1)}, u32[]{:S(2)}, u32[]{:S(2)}) %all-to-all-start.2) | async-done | bytes 131104 | tf_op jit(solution)/shard_map/all_to_all | solution.py:368
  88.2 0.0 copy-done.1
  88.2 1.9 %result.1 = f32[800,128]{1,0:T(8,128)} custom-call(f32[256,128]{1,0:T(8,128)S(1)} %bitcast.16, f32[10,64,640]{2,1,0:T(8,128)S(1)} %copy-done.1, s32[10]{0:T(128)} %dynamic_slice.3.order_ref), custom_call_target="tpu_custom_call" | custom-call | tf_op jit(solution)/shard_map/result/pallas_call | solution.py:371
Async XLA Ops:
  0.0 56.6 %copy-start.4 = (s32[640]{0:T(1024)S(1)}, s32[640]{0:T(1024)}, u32[]{:S(2)}) copy-start(s32[640]{0:T(1024)} %param.9) | copy-start | bytes 7684
  1.5 1.4 %copy-start = (f32[10,64,640]{2,1,0:T(8,128)S(1)}, f32[10,64,640]{2,1,0:T(8,128)}, u32[]{:S(2)}) copy-start(f32[10,64,640]{2,1,0:T(8,128)} %leg_ref.3) | copy-start | bytes 4915204
  3.0 0.9 copy-start.2
  3.9 43.4 %copy-start.3 = (f32[8,1,1,1280]{3,2,1,0:T(1,128)S(1)}, f32[8,1,1,1280]{3,2,1,0:T(1,128)}, u32[]{:S(2)}) copy-start(f32[8,1,1,1280]{3,2,1,0:T(1,128)} %param.13) | copy-start | bytes 122884
  3.9 84.3 %copy-start.1 = (f32[10,64,640]{2,1,0:T(8,128)S(1)}, f32[10,64,640]{2,1,0:T(8,128)}, u32[]{:S(2)}) copy-start(f32[10,64,640]{2,1,0:T(8,128)} %leg_ref.3) | copy-start | bytes 4915204
  6.0 28.4 %all-to-all-start = ((f32[16,1,1280]{2,1,0:T(1,128)}), f32[16,1,1280]{2,1,0:T(1,128)S(1)}, u32[]{:S(2)}, u32[]{:S(2)}) async-start(f32[16,1,1280]{2,1,0:T(1,128)} %bitcast.2), calls=%async_computation | async-start | bytes 163840 | tf_op jit(solution)/shard_map/all_to_all | solution.py:322
  35.2 30.3 %all-to-all-start.1 = ((f32[64,1,128]{2,1,0:T(1,128)}), f32[64,1,128]{2,1,0:T(1,128)S(1)}, u32[]{:S(2)}, u32[]{:S(2)}) async-start(f32[64,1,128]{2,1,0:T(1,128)} %bitcast.6), calls=%async_computation.1 | async-start | bytes 65536 | tf_op jit(solution)/shard_map/all_to_all | solution.py:345
  47.2 11.5 %collective-permute-start.1 = (f32[8,1,1,1280]{3,2,1,0:T(1,128)S(1)}, f32[8,1,1,1280]{3,2,1,0:T(1,128)S(1)}, u32[]{:S(2)}, u32[]{:S(2)}) collective-permute-start(f32[8,1,1,1280]{3,2,1,0:T(1,128)S(1)} %copy-done.3), channel_id=1, source_target_pairs={{1,0},{2,1},{3,2},{4,3},{5,4},{6,5},{7,6},{8,7},{9,8},{10,9},{11,1... | collective-permute-start | bytes 122888 | tf_op jit(solution)/shard_map/ppermute | solution.py:307
  54.7 10.8 %collective-permute-start = (f32[8,1,1,1280]{3,2,1,0:T(1,128)S(1)}, f32[8,1,1,1280]{3,2,1,0:T(1,128)S(1)}, u32[]{:S(2)}, u32[]{:S(2)}) collective-permute-start(f32[8,1,1,1280]{3,2,1,0:T(1,128)S(1)} %copy-done.3), channel_id=1, source_target_pairs={{0,1},{1,2},{2,3},{3,4},{4,5},{5,6},{6,7},{7,8},{8,9},{9,10},{10,1... | collective-permute-start | bytes 122888 | tf_op jit(solution)/shard_map/ppermute | solution.py:306
  67.2 21.0 %all-to-all-start.2 = ((f32[64,4,128]{2,1,0:T(4,128)}), f32[64,4,128]{2,1,0:T(4,128)S(1)}, u32[]{:S(2)}, u32[]{:S(2)}) async-start(f32[64,4,128]{2,1,0:T(4,128)} %bitcast.11), calls=%async_computation.2 | async-start | bytes 262144 | tf_op jit(solution)/shard_map/all_to_all | solution.py:368
where the time goes:
time: 90.6 us; the launch traced here: 90.2 us
  starting transfers between devices  55 us (61%)
  waiting for transfers between devices  21.9 us (24%)
  Pallas kernels  7.25 us (8%)
  local copies, waits for them, and re-layouts  3.95 us (4%)
  between operations  2.05 us (2%)
    all_to_all x1, starting transfers between devices, shards(): lax.all_to_all(message.reshape(levels, 1, slots * 128), 'lev', split_axis...  21.5 us
    all_to_all x1, starting transfers between devices, shards(): lax.all_to_all(spectra.reshape(waves, 4, 128), 'wave', split_axis=0, conc...  12.2 us
    all_to_all x1, starting transfers between devices, shards(): lax.all_to_all(sent.reshape(rows, 1, 128), 'wave', split_axis=0, concat_a...  12 us
    all_to_all x1, waiting for transfers between devices, shards(): lax.all_to_all(spectra.reshape(waves, 4, 128), 'wave', split_axis=0, conc...  8.21 us
    ppermute x1, starting transfers between devices, shards(): below = lax.ppermute(tracers, 'lev', down)  7.44 us
    all_to_all x1, waiting for transfers between devices, shards(): lax.all_to_all(message.reshape(levels, 1, slots * 128), 'lev', split_axis...  6.92 us
    ppermute x1, waiting for transfers between devices, shards(): above = lax.ppermute(tracers, 'lev', up)  6.72 us
    unnamed x10, local copies, waits for them, and re-layouts  2.33 us
  transfers between devices with their start and end apart: 5, of which 3 were waited for; matrix products, arithmetic and copies ran while one was open for 1% of the time, Pallas kernels for 1%

commit v1 on v0

--- a/solution.py
+++ b/solution.py
@@ -7,12 +7,14 @@
 from jax.experimental.pallas import tpu as pltpu
 from jax.sharding import PartitionSpec as P
 
+
 planet_radius = 20.0
 INTERPRET = False
 f32 = jnp.float32
 bf16 = jnp.bfloat16
 
 vmem = pl.BlockSpec(memory_space=pltpu.VMEM)
+hbm = pl.BlockSpec(memory_space=pl.ANY)
 smem = pl.BlockSpec(memory_space=pltpu.SMEM)
 
 
@@ -55,11 +57,45 @@
     )
 
 
-def winds_kernel(vort_ref, leg_ref, order_ref, thick_ref, f_ref, lev_ref, ft_ref, msg_ref):
+def own_orders(owner_ref, slots):
+    start = lax.axis_index("wave") * slots if not INTERPRET else owner_ref[owner_ref.shape[0] - 1] * slots
+    return [owner_ref[start + s] for s in range(slots)]
+
+
+def winds_kernel(
+    vort_hbm,
+    leg_hbm,
+    owner_hbm,
+    thick_ref,
+    f_ref,
+    lev_ref,
+    high_ref,
+    low_ref,
+    vort_ref,
+    leg_ref,
+    owner_ref,
+    ft_ref,
+    msg_ref,
+    sem,
+    leg_sem,
+):
     slots, rows, degrees = leg_ref.shape
     copies = lev_ref.shape[0] // slots
     tiles = degrees // 128
-    order = order_ref[...].astype(f32)
+    vort_copy = pltpu.make_async_copy(vort_hbm, vort_ref, sem.at[0])
+    owner_copy = pltpu.make_async_copy(owner_hbm, owner_ref, sem.at[1])
+    owner_copy.start()
+    vort_copy.start()
+    leg_copies = []
+    for s in range(slots):
+        leg_copies.append(pltpu.make_async_copy(leg_hbm.at[s], leg_ref.at[s], leg_sem.at[s]))
+        leg_copies[s].start()
+    owner_copy.wait()
+    own = own_orders(owner_ref, slots)
+    row = lax.broadcasted_iota(jnp.int32, (slots, degrees), 0)
+    order = jnp.zeros((slots, degrees), f32)
+    for s in range(slots):
+        order = jnp.where(row == s, own[s].astype(f32), order)
 
     def vort(part):
         start = part * slots * tiles
@@ -88,6 +124,7 @@
         upper = jnp.where(last, 0.0, pltpu.roll(field, degrees - 1, 1))
         return lower_factor * lower + upper_factor * upper
 
+    vort_copy.wait()
     div_real = vort(2)
     div_imag = vort(3)
     stream_real = inverse * vort(0)
@@ -118,7 +155,12 @@
         if lane + 8 < 128:
             parts.append(jnp.zeros((128 - lane - 8, degrees), f32))
         block_high, block_low = halves(jnp.concatenate(parts, axis=0))
-        total = total + three_products(leg_ref[s], block_high, block_low, dot_nt)
+        leg_copies[s].wait()
+        leg_high, leg_low = halves(leg_ref[s])
+        high_ref[s * rows : (s + 1) * rows, :] = leg_high
+        low_ref[s * rows : (s + 1) * rows, :] = leg_low
+        both = dot_nt(jnp.concatenate([leg_high, leg_low], axis=0), block_high)
+        total = total + (both[:rows] + both[rows:] + dot_nt(leg_high, block_low))
     f_ref[...] = total
     ft_ref[...] = total.T
     for s in range(slots):
@@ -218,7 +260,7 @@
     merid_factor = weight / (metric * (2.0 * lat_step))
     vertical_factor = weight / (2.0 * thick_ref[0])
     lane = lax.broadcasted_iota(jnp.int32, (8, 128), 1)
-    tracer, east, other, merid = [], [], [], []
+    east, other, merid = [], [], []
     for b in range(used):
         q = q_ref[pl.ds(b, 8, stride=used), :]
         above = above_ref[pl.ds(b, 8, stride=used), :]
@@ -255,9 +297,12 @@
             out_ref[pl.ds(kind * 2 + parity, waves, stride=4), :] = sent[parity * 64 : parity * 64 + waves]
 
 
-def result_kernel(got_ref, leg_ref, order_ref, out_ref):
-    slots, rows, degrees = leg_ref.shape
+def result_kernel(got_ref, high_ref, low_ref, owner_ref, out_ref):
+    degrees = high_ref.shape[1]
+    rows = got_ref.shape[0] // 4
+    slots = high_ref.shape[0] // rows
     tiles = degrees // 128
+    own = own_orders(owner_ref, slots)
     zero_row = jnp.zeros((1, 128), f32)
     parts = []
     for parity in range(2):
@@ -273,12 +318,11 @@
     for t in range(slots // 2):
         block = stacked[16 * t : 16 * t + 16]
         left = jnp.concatenate([jnp.where(first, block, 0.0), jnp.where(first, 0.0, block)], axis=0)
-        right = leg_ref[2 * t : 2 * t + 2].reshape(2 * rows, degrees)
-        right_high, right_low = halves(right)
-        product = three_products(left, right_high, right_low, dot_nn)
+        pair = slice(2 * t * rows, 2 * (t + 1) * rows)
+        product = three_products(left, high_ref[pair, :], low_ref[pair, :], dot_nn)
         for parity in range(2):
             s = 2 * t + parity
-            valid = degree >= order_ref[s]
+            valid = degree >= own[s]
             for part in range(2):
                 row = parity * 16 + part * 8
                 kept = jnp.where(valid, product[row : row + 8], 0.0)
@@ -305,20 +349,31 @@
     down = [(b, a) for a, b in up]
     above = lax.ppermute(tracers, "lev", up)
     below = lax.ppermute(tracers, "lev", down)
-    legendre = local(legendre)
-    own = lax.dynamic_slice_in_dim(owner_map, lax.axis_index("wave") * slots, slots)
+    owner = owner_map
+    if INTERPRET:
+        owner = jnp.concatenate([owner_map, lax.axis_index("wave").reshape(1)])
     level = lax.axis_index("lev").astype(jnp.int32).reshape(1)
-    fourier, message = call(
+    fourier, message, leg_high, leg_low = call(
         winds_kernel,
         name="winds",
-        in_specs=[vmem, vmem, vmem, smem],
-        out_specs=(vmem, vmem),
+        in_specs=[hbm, hbm, hbm, smem],
+        out_specs=(vmem, vmem, vmem, vmem),
         out_shape=(
             shaped((rows, 128)),
             shaped((levels * slots, 128)),
+            shaped((slots * rows, degrees), bf16),
+            shaped((slots * rows, degrees), bf16),
         ),
-        scratch_shapes=[pltpu.VMEM((128, rows), f32), pltpu.VMEM((slots, 128), f32)],
-    )(local(vort_div.reshape(4 * slots * degrees // 128, 128)), legendre, local(own.reshape(slots, 1)), thickness)
+        scratch_shapes=[
+            pltpu.VMEM((4 * slots * degrees // 128, 128), f32),
+            pltpu.VMEM((slots, rows, degrees), f32),
+            pltpu.SMEM(owner.shape, jnp.int32),
+            pltpu.VMEM((128, rows), f32),
+            pltpu.VMEM((slots, 128), f32),
+            pltpu.SemaphoreType.DMA((2,)),
+            pltpu.SemaphoreType.DMA((slots,)),
+        ],
+    )(vort_div.reshape(4 * slots * degrees // 128, 128), legendre, owner, thickness)
     totals = lax.all_to_all(
         message.reshape(levels, 1, slots * 128), "lev", split_axis=0, concat_axis=0, tiled=True
     ).reshape(levels * slots, 128)
@@ -371,10 +426,10 @@
     result = call(
         result_kernel,
         name="result",
-        in_specs=[vmem, vmem, smem],
+        in_specs=[vmem, vmem, vmem, smem],
         out_specs=vmem,
         out_shape=jax.ShapeDtypeStruct((count * 2 * slots * degrees // 128, 128), f32),
-    )(local(back), legendre, own)
+    )(local(back), local(leg_high), local(leg_low), owner)
     return result.reshape(count, 2, 1, slots, degrees)
 
 
@@ -388,6 +443,7 @@
         P("lev"),
         P(None, "lev", "wave", None),
     )
+
     return jax.shard_map(
         shards,
         mesh=mesh,

time: 90.6 us -> 83.7 us (0.924)
  blocking collectives: 0 us -> 19.9 us
  waiting for transfers between devices: 21.9 us -> 6.93 us
  starting transfers between devices: 55 us -> 44.9 us
  local copies, waits for them, and re-layouts: 3.95 us -> 0.13 us
  Pallas kernels: 7.25 us -> 9.42 us
    all_to_all x0 -> x1, blocking collectives: none -> 19.9 us  [shards(): lax.all_to_all(spectra.reshape(waves, 4, 128), 'wave', split_axis=0, conc...]
    all_to_all x1 -> x0, starting transfers between devices: 12.2 us -> none  [shards(): lax.all_to_all(spectra.reshape(waves, 4, 128), 'wave', split_axis=0, conc...]
    all_to_all x1 -> x0, waiting for transfers between devices: 8.21 us -> none  [shards(): lax.all_to_all(spectra.reshape(waves, 4, 128), 'wave', split_axis=0, conc...]
    ppermute x1, waiting for transfers between devices: 6.72 us -> 0.01 us  [shards(): above = lax.ppermute(tracers, 'lev', up)]
    pallas_call x2, Pallas kernels: 4.04 us -> 6.85 us  [the longest x1 4.89 us: shards(): call(winds_kernel, name='winds', in_specs=[hbm, hbm, hbm, smem], out_spec...]
    unnamed x10 -> x4, local copies, waits for them, and re-layouts: 2.33 us -> 0.01 us
    ppermute x1, starting transfers between devices: 7.44 us -> 8.66 us  [shards(): below = lax.ppermute(tracers, 'lev', down)]
  transfers between devices with their start and end apart: 5 -> 4, of which waited for: 3 -> 1; matrix products, arithmetic and copies ran while one was open for 1% -> 0% of each run, Pallas kernels for 1% -> 1%
where the time goes in v1:
time: 83.7 us; the launch traced here: 83.3 us
  starting transfers between devices  44.9 us (54%)
  blocking collectives  19.9 us (24%)
  Pallas kernels  9.42 us (11%)
  waiting for transfers between devices  6.93 us (8%)
  between operations  2.07 us (2%)
    all_to_all x1, starting transfers between devices, shards(): lax.all_to_all(message.reshape(levels, 1, slots * 128), 'lev', split_axis...  21.5 us
    all_to_all x1, blocking collectives, shards(): lax.all_to_all(spectra.reshape(waves, 4, 128), 'wave', split_axis=0, conc...  19.9 us
    all_to_all x1, starting transfers between devices, shards(): lax.all_to_all(sent.reshape(rows, 1, 128), 'wave', split_axis=0, concat_a...  12 us
    ppermute x1, starting transfers between devices, shards(): below = lax.ppermute(tracers, 'lev', down)  8.66 us
    all_to_all x1, waiting for transfers between devices, shards(): lax.all_to_all(message.reshape(levels, 1, slots * 128), 'lev', split_axis...  6.92 us
    pallas_call x1, Pallas kernels, shards(): call(winds_kernel, name='winds', in_specs=[hbm, hbm, hbm, smem], out_spec...  4.89 us
    ppermute x1, starting transfers between devices, shards(): above = lax.ppermute(tracers, 'lev', up)  2.64 us
    pallas_call x1, Pallas kernels, shards(): call(result_kernel, name='result', in_specs=[vmem, vmem, vmem, smem], out...  1.96 us
  transfers between devices with their start and end apart: 4, of which 1 were waited for; matrix products, arithmetic and copies ran while one was open for 0% of the time, Pallas kernels for 1%

profile of v1, /device:TPU:113, one launch (start us, length us, event | category | flops | bytes accessed | tf_op | source)
XLA Modules:
  0.0 83.3 jit_solution(15442906837212118660)
XLA Ops:
  0.0 0.0 copy-start.1
  0.0 0.0 copy-start
  0.7 4.9 %winds.1 = (f32[64,128]{1,0:T(8,128)S(1)}, f32[160,128]{1,0:T(8,128)}, bf16[640,640]{1,0:T(8,128)(2,1)S(1)}, bf16[640,640]{1,0:T(8,128)(2,1)S(1)}) custom-call(f32[200,128]{1,0:T(8,128)} %bitcast.21, f32[10,64,640]{2,1,0:T(8,128)} %leg_hbm.1, s32[640]{0:T(1024)} %owner_ref.1, f32[1]{0:T(128)S(6)} %copy.15.thick_ref), custom_call_target="tpu_custom_call" | custom-call | tf_op jit(solution)/shard_map/winds/pallas_call | solution.py:356
  5.6 21.5 %all-to-all-start = ((f32[16,1,1280]{2,1,0:T(1,128)}), f32[16,1,1280]{2,1,0:T(1,128)S(1)}, u32[]{:S(2)}, u32[]{:S(2)}) async-start(f32[16,1,1280]{2,1,0:T(1,128)} %bitcast.1), calls=%async_computation | async-start | bytes 163840 | tf_op jit(solution)/shard_map/all_to_all | solution.py:377
  27.1 6.9 %all-to-all-done = f32[16,1,1280]{2,1,0:T(1,128)S(1)} async-done(((f32[16,1,1280]{2,1,0:T(1,128)}), f32[16,1,1280]{2,1,0:T(1,128)S(1)}, u32[]{:S(2)}, u32[]{:S(2)}) %all-to-all-start) | async-done | bytes 81952 | tf_op jit(solution)/shard_map/all_to_all | solution.py:377
  34.0 0.8 prefix.1
  34.8 12.0 %all-to-all-start.1 = ((f32[64,1,128]{2,1,0:T(1,128)}), f32[64,1,128]{2,1,0:T(1,128)S(1)}, u32[]{:S(2)}, u32[]{:S(2)}) async-start(f32[64,1,128]{2,1,0:T(1,128)} %bitcast.5), calls=%async_computation.1 | async-start | bytes 65536 | tf_op jit(solution)/shard_map/all_to_all | solution.py:400
  46.9 0.0 copy-done
  46.9 2.6 %collective-permute-start = (f32[8,1,1,1280]{3,2,1,0:T(1,128)S(1)}, f32[8,1,1,1280]{3,2,1,0:T(1,128)S(1)}, u32[]{:S(2)}, u32[]{:S(2)}) collective-permute-start(f32[8,1,1,1280]{3,2,1,0:T(1,128)S(1)} %copy-done), channel_id=1, source_target_pairs={{0,1},{1,2},{2,3},{3,4},{4,5},{5,6},{6,7},{7,8},{8,9},{9,10},{10,1... | collective-permute-start | bytes 122888 | tf_op jit(solution)/shard_map/ppermute | solution.py:350
  49.5 8.7 %collective-permute-start.1 = (f32[8,1,1,1280]{3,2,1,0:T(1,128)S(1)}, f32[8,1,1,1280]{3,2,1,0:T(1,128)S(1)}, u32[]{:S(2)}, u32[]{:S(2)}) collective-permute-start(f32[8,1,1,1280]{3,2,1,0:T(1,128)S(1)} %copy-done), channel_id=1, source_target_pairs={{1,0},{2,1},{3,2},{4,3},{5,4},{6,5},{7,6},{8,7},{9,8},{10,9},{11,1... | collective-permute-start | bytes 122888 | tf_op jit(solution)/shard_map/ppermute | solution.py:351
  58.2 0.0 copy-done.1
  58.2 0.1 reshape.45.owner_ref
  58.3 0.7 tables.1
  60.3 0.0 collective-permute-done
  60.3 0.0 collective-permute-done.1
  60.3 0.0 all-to-all-done.1
  60.3 1.1 %grid.1 = f32[256,128]{1,0:T(8,128)S(1)} custom-call(f32[64,128]{1,0:T(8,128)S(1)} %bitcast.17, bf16[640,256]{1,0:T(8,128)(2,1)S(1)} %get-tuple-element.15.table_high_ref, bf16[640,256]{1,0:T(8,128)(2,1)S(1)} %get-tuple-element.16.table_low_ref, f32[80,128]{1,0:T(8,128)S(1)} %get-tuple-element.17.phase_cos_ref, ...), custom_call_target="tpu_custom_call" | custom-call | tf_op jit(solution)/shard_map/grid/pallas_call | solution.py:404
  61.4 19.9 %all_to_all.15 = f32[64,4,128]{2,1,0:T(4,128)S(1)} all-to-all(f32[64,4,128]{2,1,0:T(4,128)S(1)} %bitcast.14), channel_id=1, replica_groups=mesh['wave'=64,'lev'=16] {'wave'}, dimensions={0} | all-to-all | bytes 262144 | tf_op jit(solution)/shard_map/all_to_all | solution.py:423
  81.4 2.0 %result.1 = f32[800,128]{1,0:T(8,128)} custom-call(f32[256,128]{1,0:T(8,128)S(1)} %bitcast.15, bf16[640,640]{1,0:T(8,128)(2,1)S(1)} %get-tuple-element.19.high_ref, bf16[640,640]{1,0:T(8,128)(2,1)S(1)} %get-tuple-element.20.low_ref, s32[640]{0:T(1024)} %owner_ref.1), custom_call_target="tpu_custom_call" | custom-call | tf_op jit(solution)/shard_map/result/pallas_call | solution.py:426
Async XLA Ops:
  0.0 58.2 %copy-start.1 = (s32[640]{0:T(1024)S(1)}, s32[640]{0:T(1024)}, u32[]{:S(2)}) copy-start(s32[640]{0:T(1024)} %owner_ref.1) | copy-start | bytes 7684
  0.0 46.9 %copy-start = (f32[8,1,1,1280]{3,2,1,0:T(1,128)S(1)}, f32[8,1,1,1280]{3,2,1,0:T(1,128)}, u32[]{:S(2)}) copy-start(f32[8,1,1,1280]{3,2,1,0:T(1,128)} %param.13) | copy-start | bytes 122884
  5.6 28.4 %all-to-all-start = ((f32[16,1,1280]{2,1,0:T(1,128)}), f32[16,1,1280]{2,1,0:T(1,128)S(1)}, u32[]{:S(2)}, u32[]{:S(2)}) async-start(f32[16,1,1280]{2,1,0:T(1,128)} %bitcast.1), calls=%async_computation | async-start | bytes 163840 | tf_op jit(solution)/shard_map/all_to_all | solution.py:377
  34.8 25.5 %all-to-all-start.1 = ((f32[64,1,128]{2,1,0:T(1,128)}), f32[64,1,128]{2,1,0:T(1,128)S(1)}, u32[]{:S(2)}, u32[]{:S(2)}) async-start(f32[64,1,128]{2,1,0:T(1,128)} %bitcast.5), calls=%async_computation.1 | async-start | bytes 65536 | tf_op jit(solution)/shard_map/all_to_all | solution.py:400
  46.9 13.4 %collective-permute-start = (f32[8,1,1,1280]{3,2,1,0:T(1,128)S(1)}, f32[8,1,1,1280]{3,2,1,0:T(1,128)S(1)}, u32[]{:S(2)}, u32[]{:S(2)}) collective-permute-start(f32[8,1,1,1280]{3,2,1,0:T(1,128)S(1)} %copy-done), channel_id=1, source_target_pairs={{0,1},{1,2},{2,3},{3,4},{4,5},{5,6},{6,7},{7,8},{8,9},{9,10},{10,1... | collective-permute-start | bytes 122888 | tf_op jit(solution)/shard_map/ppermute | solution.py:350
  49.5 10.8 %collective-permute-start.1 = (f32[8,1,1,1280]{3,2,1,0:T(1,128)S(1)}, f32[8,1,1,1280]{3,2,1,0:T(1,128)S(1)}, u32[]{:S(2)}, u32[]{:S(2)}) collective-permute-start(f32[8,1,1,1280]{3,2,1,0:T(1,128)S(1)} %copy-done), channel_id=1, source_target_pairs={{1,0},{2,1},{3,2},{4,3},{5,4},{6,5},{7,6},{8,7},{9,8},{10,9},{11,1... | collective-permute-start | bytes 122888 | tf_op jit(solution)/shard_map/ppermute | solution.py:351

commit v2 on v1

--- a/solution.py
+++ b/solution.py
@@ -14,7 +14,7 @@
 bf16 = jnp.bfloat16
 
 vmem = pl.BlockSpec(memory_space=pltpu.VMEM)
-hbm = pl.BlockSpec(memory_space=pl.ANY)
+hbm = pl.BlockSpec(memory_space=pltpu.HBM)
 smem = pl.BlockSpec(memory_space=pltpu.SMEM)
 
 
@@ -66,7 +66,7 @@
     vort_hbm,
     leg_hbm,
     owner_hbm,
-    thick_ref,
+    thick_hbm,
     f_ref,
     lev_ref,
     high_ref,
@@ -74,7 +74,8 @@
     vort_ref,
     leg_ref,
     owner_ref,
-    ft_ref,
+    thick_ref,
+    field_ref,
     msg_ref,
     sem,
     leg_sem,
@@ -84,12 +85,15 @@
     tiles = degrees // 128
     vort_copy = pltpu.make_async_copy(vort_hbm, vort_ref, sem.at[0])
     owner_copy = pltpu.make_async_copy(owner_hbm, owner_ref, sem.at[1])
-    owner_copy.start()
-    vort_copy.start()
-    leg_copies = []
-    for s in range(slots):
-        leg_copies.append(pltpu.make_async_copy(leg_hbm.at[s], leg_ref.at[s], leg_sem.at[s]))
-        leg_copies[s].start()
+    thick_copy = pltpu.make_async_copy(thick_hbm, thick_ref, sem.at[2])
+    owner_copy.start(priority=1)
+    thick_copy.start(priority=1)
+    vort_copy.start(priority=1)
+
+    def leg_copy(s):
+        return pltpu.make_async_copy(leg_hbm.at[s], leg_ref.at[s], leg_sem.at[s])
+
+    lax.fori_loop(0, slots, lambda s, _: leg_copy(s).start(), None)
     owner_copy.wait()
     own = own_orders(owner_ref, slots)
     row = lax.broadcasted_iota(jnp.int32, (slots, degrees), 0)
@@ -125,6 +129,7 @@
         return lower_factor * lower + upper_factor * upper
 
     vort_copy.wait()
+    thick_copy.wait()
     div_real = vort(2)
     div_imag = vort(3)
     stream_real = inverse * vort(0)
@@ -132,7 +137,7 @@
     potential_real = inverse * div_real
     potential_imag = inverse * div_imag
     scale = 1.0 / planet_radius
-    thickness = thick_ref[0]
+    thickness = thick_ref[0, 0]
     zeros = jnp.zeros((slots, degrees), f32)
     fields = [
         (-order * potential_imag - derivative(stream_real)) * scale,
@@ -144,29 +149,40 @@
         div_imag * thickness,
         zeros,
     ]
-    fields = [jnp.where(valid, field, 0.0) for field in fields]
-    total = jnp.zeros((rows, 128), f32)
-    for s in range(slots):
-        lane = (s % 2) * 64 + (s // 2) * 8
-        block = jnp.concatenate([field[s : s + 1] for field in fields], axis=0)
-        parts = [block]
-        if lane > 0:
-            parts.insert(0, jnp.zeros((lane, degrees), f32))
-        if lane + 8 < 128:
-            parts.append(jnp.zeros((128 - lane - 8, degrees), f32))
-        block_high, block_low = halves(jnp.concatenate(parts, axis=0))
-        leg_copies[s].wait()
-        leg_high, leg_low = halves(leg_ref[s])
-        high_ref[s * rows : (s + 1) * rows, :] = leg_high
-        low_ref[s * rows : (s + 1) * rows, :] = leg_low
-        both = dot_nt(jnp.concatenate([leg_high, leg_low], axis=0), block_high)
-        total = total + (both[:rows] + both[rows:] + dot_nt(leg_high, block_low))
-    f_ref[...] = total
-    ft_ref[...] = total.T
-    for s in range(slots):
-        lane = (s % 2) * 64 + (s // 2) * 8
-        msg_ref[s : s + 1, 0:rows] = ft_ref[lane + 2 : lane + 3, :]
-        msg_ref[s : s + 1, rows : 2 * rows] = ft_ref[lane + 6 : lane + 7, :]
+    for f, field in enumerate(fields):
+        for tile in range(tiles):
+            start = 128 * tile + 16 * f
+            field_ref[start : start + slots, :] = field[:, 128 * tile : 128 * tile + 128]
+    first = lax.broadcasted_iota(jnp.int32, (8, 2 * rows), 1) < rows
+    for t in range(slots // 2):
+        blocks = [
+            jnp.concatenate(
+                [
+                    field_ref[pl.ds(128 * tile + 2 * t + parity, 8, stride=16), :]
+                    for tile in range(tiles)
+                ],
+                axis=1,
+            )
+            for parity in range(2)
+        ]
+        left = jnp.concatenate(blocks, axis=0)
+        left_low = left - left.astype(bf16).astype(f32)
+        left = jnp.concatenate([left, left_low], axis=0).astype(bf16)
+        highs, lows = [], []
+        for parity in range(2):
+            s = 2 * t + parity
+            leg_copy(s).wait()
+            leg_high, leg_low = halves(jnp.where(valid[s : s + 1], leg_ref[s], 0.0))
+            high_ref[s * rows : (s + 1) * rows, :] = leg_high
+            low_ref[s * rows : (s + 1) * rows, :] = leg_low
+            highs.append(leg_high)
+            lows.append(leg_low)
+        product = dot_nt(left, jnp.concatenate(highs + lows, axis=0))
+        total = product[0:16, 0:128] + product[0:16, 128:256] + product[16:32, 0:128]
+        total = jnp.where(first, total[0:8], total[8:16])
+        f_ref[8 * t : 8 * t + 8, :] = total
+        msg_ref[2 * t : 2 * t + 1, :] = total[2:3]
+        msg_ref[2 * t + 1 : 2 * t + 2, :] = total[6:7]
     message = msg_ref[...]
     for copy in range(copies):
         lev_ref[copy * slots : (copy + 1) * slots, :] = message
@@ -198,19 +214,20 @@
 
 
 def prefix_kernel(got_ref, f_ref, level_ref, out_ref, ft_ref):
-    rows = f_ref.shape[0]
-    slots = 10
-    copies = got_ref.shape[0] // slots
+    pairs = f_ref.shape[0] // 8
+    copies = got_ref.shape[0] // (2 * pairs)
     level = level_ref[0]
-    total = jnp.zeros((slots, 128), f32)
+    total = jnp.zeros((2 * pairs, 128), f32)
     for source in range(copies):
-        total = total + jnp.where(source < level, got_ref[source * slots : (source + 1) * slots, :], 0.0)
-    ft_ref[...] = jnp.zeros((128, rows), f32)
-    for s in range(slots):
-        lane = (s % 2) * 64 + (s // 2) * 8
-        ft_ref[lane + 3 : lane + 4, :] = total[s : s + 1, 0:rows]
-        ft_ref[lane + 7 : lane + 8, :] = total[s : s + 1, rows : 2 * rows]
-    out_ref[...] = f_ref[...] + ft_ref[...].T
+        part = got_ref[source * 2 * pairs : (source + 1) * 2 * pairs, :]
+        total = total + jnp.where(source < level, part, 0.0)
+    ft_ref[0 : 8 * pairs, :] = f_ref[...]
+    ft_ref[8 * pairs : 128, :] = jnp.zeros((128 - 8 * pairs, 128), f32)
+    for t in range(pairs):
+        ft_ref[8 * t + 3 : 8 * t + 4, :] = total[2 * t : 2 * t + 1]
+        ft_ref[8 * t + 7 : 8 * t + 8, :] = total[2 * t + 1 : 2 * t + 2]
+    turned = ft_ref[...].T
+    out_ref[...] = turned[0:64] + pltpu.roll(turned[64:128], 64, 1)
 
 
 def grid_kernel(
@@ -297,12 +314,11 @@
             out_ref[pl.ds(kind * 2 + parity, waves, stride=4), :] = sent[parity * 64 : parity * 64 + waves]
 
 
-def result_kernel(got_ref, high_ref, low_ref, owner_ref, out_ref):
+def result_kernel(got_ref, high_ref, low_ref, out_ref):
     degrees = high_ref.shape[1]
     rows = got_ref.shape[0] // 4
     slots = high_ref.shape[0] // rows
     tiles = degrees // 128
-    own = own_orders(owner_ref, slots)
     zero_row = jnp.zeros((1, 128), f32)
     parts = []
     for parity in range(2):
@@ -314,7 +330,6 @@
         parts.append(rest + factor * (north - south))
     stacked = jnp.concatenate(parts, axis=0).T
     first = lax.broadcasted_iota(jnp.int32, (16, 2 * rows), 1) < rows
-    degree = lax.broadcasted_iota(jnp.int32, (8, degrees), 1)
     for t in range(slots // 2):
         block = stacked[16 * t : 16 * t + 16]
         left = jnp.concatenate([jnp.where(first, block, 0.0), jnp.where(first, 0.0, block)], axis=0)
@@ -322,10 +337,9 @@
         product = three_products(left, high_ref[pair, :], low_ref[pair, :], dot_nn)
         for parity in range(2):
             s = 2 * t + parity
-            valid = degree >= own[s]
             for part in range(2):
                 row = parity * 16 + part * 8
-                kept = jnp.where(valid, product[row : row + 8], 0.0)
+                kept = product[row : row + 8]
                 for tile in range(tiles):
                     start = (part * slots + s) * tiles + tile
                     out_ref[pl.ds(start, 8, stride=2 * slots * tiles), :] = kept[:, 128 * tile : 128 * tile + 128]
@@ -356,10 +370,10 @@
     fourier, message, leg_high, leg_low = call(
         winds_kernel,
         name="winds",
-        in_specs=[hbm, hbm, hbm, smem],
+        in_specs=[hbm, hbm, hbm, hbm],
         out_specs=(vmem, vmem, vmem, vmem),
         out_shape=(
-            shaped((rows, 128)),
+            shaped((4 * slots, 128)),
             shaped((levels * slots, 128)),
             shaped((slots * rows, degrees), bf16),
             shaped((slots * rows, degrees), bf16),
@@ -368,12 +382,13 @@
             pltpu.VMEM((4 * slots * degrees // 128, 128), f32),
             pltpu.VMEM((slots, rows, degrees), f32),
             pltpu.SMEM(owner.shape, jnp.int32),
-            pltpu.VMEM((128, rows), f32),
+            pltpu.SMEM((1, 1), f32),
+            pltpu.VMEM((degrees, 128), f32),
             pltpu.VMEM((slots, 128), f32),
-            pltpu.SemaphoreType.DMA((2,)),
+            pltpu.SemaphoreType.DMA((3,)),
             pltpu.SemaphoreType.DMA((slots,)),
         ],
-    )(vort_div.reshape(4 * slots * degrees // 128, 128), legendre, owner, thickness)
+    )(vort_div.reshape(4 * slots * degrees // 128, 128), legendre, owner, thickness.reshape(1, 1))
     totals = lax.all_to_all(
         message.reshape(levels, 1, slots * 128), "lev", split_axis=0, concat_axis=0, tiled=True
     ).reshape(levels * slots, 128)
@@ -395,7 +410,7 @@
         in_specs=[vmem, vmem, smem],
         out_specs=vmem,
         out_shape=shaped((rows, 128)),
-        scratch_shapes=[pltpu.VMEM((128, rows), f32)],
+        scratch_shapes=[pltpu.VMEM((128, 128), f32)],
     )(local(totals), local(fourier), level)
     got = lax.all_to_all(
         sent.reshape(rows, 1, 128), "wave", split_axis=0, concat_axis=0, tiled=True
@@ -426,10 +441,10 @@
     result = call(
         result_kernel,
         name="result",
-        in_specs=[vmem, vmem, vmem, smem],
+        in_specs=[vmem, vmem, vmem],
         out_specs=vmem,
         out_shape=jax.ShapeDtypeStruct((count * 2 * slots * degrees // 128, 128), f32),
-    )(local(back), local(leg_high), local(leg_low), owner)
+    )(local(back), local(leg_high), local(leg_low))
     return result.reshape(count, 2, 1, slots, degrees)
 
 

time: 83.7 us -> 87.8 us (1.049)
  waiting for transfers between devices: 6.93 us -> 13.6 us
  starting transfers between devices: 44.9 us -> 42.9 us
  Pallas kernels: 9.42 us -> 7.86 us
  blocking collectives: 19.9 us -> 20.8 us
    ppermute x1, waiting for transfers between devices: 0.01 us -> 6.72 us  [shards(): above = lax.ppermute(tracers, 'lev', up)]
    pallas_call x2, Pallas kernels: 6.85 us -> 5.29 us  [the longest x1 4.02 us: shards(): call(winds_kernel, name='winds', in_specs=[hbm, hbm, hbm, hbm], out_specs...]
    ppermute x1, starting transfers between devices: 8.66 us -> 7.45 us  [shards(): below = lax.ppermute(tracers, 'lev', down)]
  transfers between devices with their start and end apart: 4 -> 4, of which waited for: 1 -> 2; matrix products, arithmetic and copies ran while one was open for 0% -> 0% of each run, Pallas kernels for 1% -> 1%
where the time goes in v2:
time: 87.8 us; the launch traced here: 87.4 us
  starting transfers between devices  42.9 us (49%)
  blocking collectives  20.8 us (24%)
  waiting for transfers between devices  13.6 us (15%)
  Pallas kernels  7.86 us (9%)
  between operations  2.05 us (2%)
    all_to_all x1, starting transfers between devices, shards(): lax.all_to_all(message.reshape(levels, 1, slots * 128), 'lev', split_axis...  21.5 us
    all_to_all x1, blocking collectives, shards(): lax.all_to_all(spectra.reshape(waves, 4, 128), 'wave', split_axis=0, conc...  20.8 us
    all_to_all x1, starting transfers between devices, shards(): lax.all_to_all(sent.reshape(rows, 1, 128), 'wave', split_axis=0, concat_a...  12 us
    ppermute x1, starting transfers between devices, shards(): below = lax.ppermute(tracers, 'lev', down)  7.45 us
    all_to_all x1, waiting for transfers between devices, shards(): lax.all_to_all(message.reshape(levels, 1, slots * 128), 'lev', split_axis...  6.92 us
    ppermute x1, waiting for transfers between devices, shards(): above = lax.ppermute(tracers, 'lev', up)  6.72 us
    pallas_call x1, Pallas kernels, shards(): call(winds_kernel, name='winds', in_specs=[hbm, hbm, hbm, hbm], out_specs...  4.02 us
    ppermute x1, starting transfers between devices, shards(): above = lax.ppermute(tracers, 'lev', up)  1.92 us
  transfers between devices with their start and end apart: 4, of which 2 were waited for; matrix products, arithmetic and copies ran while one was open for 0% of the time, Pallas kernels for 1%

profile of v2, /device:TPU:113, one launch (start us, length us, event | category | flops | bytes accessed | tf_op | source)
XLA Modules:
  0.0 87.4 jit_solution(5345339078079940888)
XLA Ops:
  0.0 0.0 copy-start.1
  0.0 0.0 copy-start
  0.7 4.0 %winds.1 = (f32[40,128]{1,0:T(8,128)S(1)}, f32[160,128]{1,0:T(8,128)}, bf16[640,640]{1,0:T(8,128)(2,1)S(1)}, bf16[640,640]{1,0:T(8,128)(2,1)S(1)}) custom-call(f32[200,128]{1,0:T(8,128)} %bitcast.23, f32[10,64,640]{2,1,0:T(8,128)} %leg_hbm.1, s32[640]{0:T(1024)} %owner_hbm.1, f32[1,1]{1,0:T(1,128)} %bitcast.15.thick_hbm), custom_call_target="tpu_custom_call" | custom-call | tf_op jit(solution)/shard_map/winds/pallas_call | solution.py:370
  4.7 21.5 %all-to-all-start = ((f32[16,1,1280]{2,1,0:T(1,128)}), f32[16,1,1280]{2,1,0:T(1,128)S(1)}, u32[]{:S(2)}, u32[]{:S(2)}) async-start(f32[16,1,1280]{2,1,0:T(1,128)} %bitcast.2), calls=%async_computation | async-start | bytes 163840 | tf_op jit(solution)/shard_map/all_to_all | solution.py:392
  26.2 6.9 %all-to-all-done = f32[16,1,1280]{2,1,0:T(1,128)S(1)} async-done(((f32[16,1,1280]{2,1,0:T(1,128)}), f32[16,1,1280]{2,1,0:T(1,128)S(1)}, u32[]{:S(2)}, u32[]{:S(2)}) %all-to-all-start) | async-done | bytes 81952 | tf_op jit(solution)/shard_map/all_to_all | solution.py:392
  33.2 0.8 prefix.1
  34.0 12.0 %all-to-all-start.1 = ((f32[64,1,128]{2,1,0:T(1,128)}), f32[64,1,128]{2,1,0:T(1,128)S(1)}, u32[]{:S(2)}, u32[]{:S(2)}) async-start(f32[64,1,128]{2,1,0:T(1,128)} %bitcast.6), calls=%async_computation.1 | async-start | bytes 65536 | tf_op jit(solution)/shard_map/all_to_all | solution.py:415
  46.0 0.0 copy-done
  46.0 7.4 %collective-permute-start.1 = (f32[8,1,1,1280]{3,2,1,0:T(1,128)S(1)}, f32[8,1,1,1280]{3,2,1,0:T(1,128)S(1)}, u32[]{:S(2)}, u32[]{:S(2)}) collective-permute-start(f32[8,1,1,1280]{3,2,1,0:T(1,128)S(1)} %copy-done), channel_id=1, source_target_pairs={{1,0},{2,1},{3,2},{4,3},{5,4},{6,5},{7,6},{8,7},{9,8},{10,9},{11,1... | collective-permute-start | bytes 122888 | tf_op jit(solution)/shard_map/ppermute | solution.py:365
  53.5 1.9 %collective-permute-start = (f32[8,1,1,1280]{3,2,1,0:T(1,128)S(1)}, f32[8,1,1,1280]{3,2,1,0:T(1,128)S(1)}, u32[]{:S(2)}, u32[]{:S(2)}) collective-permute-start(f32[8,1,1,1280]{3,2,1,0:T(1,128)S(1)} %copy-done), channel_id=1, source_target_pairs={{0,1},{1,2},{2,3},{3,4},{4,5},{5,6},{6,7},{7,8},{8,9},{9,10},{10,1... | collective-permute-start | bytes 122888 | tf_op jit(solution)/shard_map/ppermute | solution.py:364
  55.4 0.0 copy-done.1
  55.4 0.1 reshape.49.owner_ref
  55.5 0.7 tables.1
  57.5 0.0 collective-permute-done.1
  57.5 6.7 %collective-permute-done = f32[8,1,1,1280]{3,2,1,0:T(1,128)S(1)} collective-permute-done((f32[8,1,1,1280]{3,2,1,0:T(1,128)S(1)}, f32[8,1,1,1280]{3,2,1,0:T(1,128)S(1)}, u32[]{:S(2)}, u32[]{:S(2)}) %collective-permute-start) | collective-permute-done | bytes 40992 | tf_op jit(solution)/shard_map/ppermute | solution.py:364
  64.2 0.0 all-to-all-done.1
  64.2 1.1 %grid.1 = f32[256,128]{1,0:T(8,128)S(1)} custom-call(f32[64,128]{1,0:T(8,128)S(1)} %bitcast.19, bf16[640,256]{1,0:T(8,128)(2,1)S(1)} %get-tuple-element.15.table_high_ref, bf16[640,256]{1,0:T(8,128)(2,1)S(1)} %get-tuple-element.16.table_low_ref, f32[80,128]{1,0:T(8,128)S(1)} %get-tuple-element.17.phase_cos_ref, ...), custom_call_target="tpu_custom_call" | custom-call | tf_op jit(solution)/shard_map/grid/pallas_call | solution.py:419
  65.4 20.8 %all_to_all.15 = f32[64,4,128]{2,1,0:T(4,128)S(1)} all-to-all(f32[64,4,128]{2,1,0:T(4,128)S(1)} %bitcast.16), channel_id=1, replica_groups=mesh['wave'=64,'lev'=16] {'wave'}, dimensions={0} | all-to-all | bytes 262144 | tf_op jit(solution)/shard_map/all_to_all | solution.py:438
  86.1 1.3 %result.1 = f32[800,128]{1,0:T(8,128)} custom-call(f32[256,128]{1,0:T(8,128)S(1)} %bitcast.17, bf16[640,640]{1,0:T(8,128)(2,1)S(1)} %get-tuple-element.19.high_ref, bf16[640,640]{1,0:T(8,128)(2,1)S(1)} %get-tuple-element.20.low_ref), custom_call_target="tpu_custom_call" | custom-call | tf_op jit(solution)/shard_map/result/pallas_call | solution.py:441
Async XLA Ops:
  0.0 55.4 %copy-start.1 = (s32[640]{0:T(1024)S(1)}, s32[640]{0:T(1024)}, u32[]{:S(2)}) copy-start(s32[640]{0:T(1024)} %owner_hbm.1) | copy-start | bytes 7684
  0.0 46.0 %copy-start = (f32[8,1,1,1280]{3,2,1,0:T(1,128)S(1)}, f32[8,1,1,1280]{3,2,1,0:T(1,128)}, u32[]{:S(2)}) copy-start(f32[8,1,1,1280]{3,2,1,0:T(1,128)} %param.13) | copy-start | bytes 122884
  4.7 28.4 %all-to-all-start = ((f32[16,1,1280]{2,1,0:T(1,128)}), f32[16,1,1280]{2,1,0:T(1,128)S(1)}, u32[]{:S(2)}, u32[]{:S(2)}) async-start(f32[16,1,1280]{2,1,0:T(1,128)} %bitcast.2), calls=%async_computation | async-start | bytes 163840 | tf_op jit(solution)/shard_map/all_to_all | solution.py:392
  34.0 30.3 %all-to-all-start.1 = ((f32[64,1,128]{2,1,0:T(1,128)}), f32[64,1,128]{2,1,0:T(1,128)S(1)}, u32[]{:S(2)}, u32[]{:S(2)}) async-start(f32[64,1,128]{2,1,0:T(1,128)} %bitcast.6), calls=%async_computation.1 | async-start | bytes 65536 | tf_op jit(solution)/shard_map/all_to_all | solution.py:415
  46.0 11.5 %collective-permute-start.1 = (f32[8,1,1,1280]{3,2,1,0:T(1,128)S(1)}, f32[8,1,1,1280]{3,2,1,0:T(1,128)S(1)}, u32[]{:S(2)}, u32[]{:S(2)}) collective-permute-start(f32[8,1,1,1280]{3,2,1,0:T(1,128)S(1)} %copy-done), channel_id=1, source_target_pairs={{1,0},{2,1},{3,2},{4,3},{5,4},{6,5},{7,6},{8,7},{9,8},{10,9},{11,1... | collective-permute-start | bytes 122888 | tf_op jit(solution)/shard_map/ppermute | solution.py:365
  53.5 10.8 %collective-permute-start = (f32[8,1,1,1280]{3,2,1,0:T(1,128)S(1)}, f32[8,1,1,1280]{3,2,1,0:T(1,128)S(1)}, u32[]{:S(2)}, u32[]{:S(2)}) collective-permute-start(f32[8,1,1,1280]{3,2,1,0:T(1,128)S(1)} %copy-done), channel_id=1, source_target_pairs={{0,1},{1,2},{2,3},{3,4},{4,5},{5,6},{6,7},{7,8},{8,9},{9,10},{10,1... | collective-permute-start | bytes 122888 | tf_op jit(solution)/shard_map/ppermute | solution.py:364

commit v3 on v2

--- a/solution.py
+++ b/solution.py
@@ -78,7 +78,6 @@
     field_ref,
     msg_ref,
     sem,
-    leg_sem,
 ):
     slots, rows, degrees = leg_ref.shape
     copies = lev_ref.shape[0] // slots
@@ -90,10 +89,8 @@
     thick_copy.start(priority=1)
     vort_copy.start(priority=1)
 
-    def leg_copy(s):
-        return pltpu.make_async_copy(leg_hbm.at[s], leg_ref.at[s], leg_sem.at[s])
-
-    lax.fori_loop(0, slots, lambda s, _: leg_copy(s).start(), None)
+    leg_copy = pltpu.make_async_copy(leg_hbm, leg_ref, sem.at[3])
+    leg_copy.start()
     owner_copy.wait()
     own = own_orders(owner_ref, slots)
     row = lax.broadcasted_iota(jnp.int32, (slots, degrees), 0)
@@ -130,6 +127,7 @@
 
     vort_copy.wait()
     thick_copy.wait()
+    leg_copy.wait()
     div_real = vort(2)
     div_imag = vort(3)
     stream_real = inverse * vort(0)
@@ -171,7 +169,6 @@
         highs, lows = [], []
         for parity in range(2):
             s = 2 * t + parity
-            leg_copy(s).wait()
             leg_high, leg_low = halves(jnp.where(valid[s : s + 1], leg_ref[s], 0.0))
             high_ref[s * rows : (s + 1) * rows, :] = leg_high
             low_ref[s * rows : (s + 1) * rows, :] = leg_low
@@ -188,7 +185,17 @@
         lev_ref[copy * slots : (copy + 1) * slots, :] = message
 
 
-def table_kernel(owner_ref, table_high_ref, table_low_ref, phase_cos_ref, phase_sin_ref):
+def table_kernel(
+    owner_ref,
+    sine_ref,
+    weight_ref,
+    thick_ref,
+    table_high_ref,
+    table_low_ref,
+    phase_cos_ref,
+    phase_sin_ref,
+    factor_ref,
+):
     waves, slots = owner_ref.shape
     length = 2.0 * waves * slots
     orders = owner_ref[...].astype(f32)
@@ -211,23 +218,45 @@
         cosine, sine = cos_sin(row * block * 128.0, length / 4.0)
         phase_cos_ref[t * blocks : (t + 1) * blocks, :] = cosine
         phase_sin_ref[t * blocks : (t + 1) * blocks, :] = sine
-
-
-def prefix_kernel(got_ref, f_ref, level_ref, out_ref, ft_ref):
+    step = 2.0 * math.pi / length
+    sine = sine_ref[0]
+    weight = jnp.full((8, 128), -weight_ref[0] * (2.0 / length), f32)
+    slope = weight / ((1.0 - sine * sine) * (2.0 * step))
+    factor_ref[0:8, :] = slope
+    factor_ref[8:16, :] = slope
+    factor_ref[16:24, :] = weight / (2.0 * thick_ref[0])
+
+
+def prefix_kernel(got_ref, f_ref, *rest):
+    level_ref, out_ref, ft_ref = rest if INTERPRET else (None, *rest)
+    level = level_ref[0] if INTERPRET else lax.axis_index("lev")
     pairs = f_ref.shape[0] // 8
-    copies = got_ref.shape[0] // (2 * pairs)
-    level = level_ref[0]
-    total = jnp.zeros((2 * pairs, 128), f32)
-    for source in range(copies):
+    depth = got_ref.shape[0] // (2 * pairs)
+    half = level // depth
+    own_sum = jnp.zeros((2 * pairs, 128), f32)
+    all_sum = jnp.zeros((2 * pairs, 128), f32)
+    for source in range(depth):
         part = got_ref[source * 2 * pairs : (source + 1) * 2 * pairs, :]
-        total = total + jnp.where(source < level, part, 0.0)
-    ft_ref[0 : 8 * pairs, :] = f_ref[...]
-    ft_ref[8 * pairs : 128, :] = jnp.zeros((128 - 8 * pairs, 128), f32)
-    for t in range(pairs):
-        ft_ref[8 * t + 3 : 8 * t + 4, :] = total[2 * t : 2 * t + 1]
-        ft_ref[8 * t + 7 : 8 * t + 8, :] = total[2 * t + 1 : 2 * t + 2]
-    turned = ft_ref[...].T
-    out_ref[...] = turned[0:64] + pltpu.roll(turned[64:128], 64, 1)
+        own_sum = own_sum + jnp.where(source < level - half * depth, part, 0.0)
+        all_sum = all_sum + part
+    to_upper = jnp.where(half == 0, all_sum, 0.0)
+    blocks = []
+    for block, total in enumerate((own_sum, to_upper)):
+        start = 128 * block
+        if block == 0:
+            ft_ref[start : start + 8 * pairs, :] = f_ref[...]
+            ft_ref[start + 8 * pairs : start + 128, :] = jnp.zeros((128 - 8 * pairs, 128), f32)
+        else:
+            ft_ref[start : start + 128, :] = jnp.zeros((128, 128), f32)
+        for t in range(pairs):
+            row = start + 8 * t
+            ft_ref[row + 3 : row + 4, :] = total[2 * t : 2 * t + 1]
+            ft_ref[row + 7 : row + 8, :] = total[2 * t + 1 : 2 * t + 2]
+        turned = ft_ref[start : start + 128, :].T
+        blocks.append(turned[0:64] + pltpu.roll(turned[64:128], 64, 1))
+    own_block, other_block = blocks
+    out_ref[0:64, :] = jnp.where(half == 0, own_block, other_block)
+    out_ref[64:128, :] = jnp.where(half == 0, other_block, own_block)
 
 
 def grid_kernel(
@@ -239,16 +268,14 @@
     q_ref,
     above_ref,
     below_ref,
-    sine_ref,
-    weight_ref,
-    thick_ref,
+    factor_ref,
     out_ref,
 ):
-    waves = got_ref.shape[0]
+    waves = got_ref.shape[0] // 2
     pairs = 5
     blocks = phase_cos_ref.shape[0] // pairs
     used = q_ref.shape[0] // 8
-    got = got_ref[...]
+    got = got_ref[0:waves, :] + got_ref[waves : 2 * waves, :]
     stacked = jnp.concatenate([got, pltpu.roll(got, 64, 1)], axis=0).T
     sign = jnp.where(lax.broadcasted_iota(jnp.int32, (8, 128), 0) < 4, -1.0, 1.0)
     plain = [stacked[8 * t : 8 * t + 8] for t in range(pairs)]
@@ -267,15 +294,9 @@
     table_high = table_high_ref[...]
     table_low = table_low_ref[...]
     grid = three_products(turned, table_high, table_low, dot_nn)
-    length = 128.0 * used
-    lon_step = 2.0 * math.pi / length
-    lat_step = 2.0 * math.pi / length
-    sine = sine_ref[0]
-    metric = 1.0 - sine * sine
-    weight = -weight_ref[0] * (2.0 / length)
-    zonal_factor = weight / (metric * (2.0 * lon_step))
-    merid_factor = weight / (metric * (2.0 * lat_step))
-    vertical_factor = weight / (2.0 * thick_ref[0])
+    zonal_factor = factor_ref[0:8, :]
+    merid_factor = factor_ref[8:16, :]
+    vertical_factor = factor_ref[16:24, :]
     lane = lax.broadcasted_iota(jnp.int32, (8, 128), 1)
     east, other, merid = [], [], []
     for b in range(used):
@@ -308,7 +329,7 @@
                 cos_total = cos_total + phase_cos[b][t] * c + phase_sin[b][t] * s
                 sin_total = sin_total + phase_cos[b][t] * s - phase_sin[b][t] * c
             stack += [cos_total, sin_total]
-        stack.append(jnp.full((128 - 16 * pairs, 128), merid_factor, f32))
+        stack += [merid_factor] * (16 - 2 * pairs)
         sent = jnp.concatenate(stack, axis=0).T
         for parity in range(2):
             out_ref[pl.ds(kind * 2 + parity, waves, stride=4), :] = sent[parity * 64 : parity * 64 + waves]
@@ -366,7 +387,12 @@
     owner = owner_map
     if INTERPRET:
         owner = jnp.concatenate([owner_map, lax.axis_index("wave").reshape(1)])
-    level = lax.axis_index("lev").astype(jnp.int32).reshape(1)
+    depth = levels // 2
+    columns = [[half * depth + z for z in range(depth)] for half in range(2)]
+    planes = [
+        [w * levels + half * depth + z for half in range(2) for w in range(waves)] for z in range(depth)
+    ]
+    level = (lax.axis_index("lev").reshape(1),) if INTERPRET else ()
     fourier, message, leg_high, leg_low = call(
         winds_kernel,
         name="winds",
@@ -374,7 +400,7 @@
         out_specs=(vmem, vmem, vmem, vmem),
         out_shape=(
             shaped((4 * slots, 128)),
-            shaped((levels * slots, 128)),
+            shaped((depth * slots, 128)),
             shaped((slots * rows, degrees), bf16),
             shaped((slots * rows, degrees), bf16),
         ),
@@ -385,41 +411,51 @@
             pltpu.SMEM((1, 1), f32),
             pltpu.VMEM((degrees, 128), f32),
             pltpu.VMEM((slots, 128), f32),
-            pltpu.SemaphoreType.DMA((3,)),
-            pltpu.SemaphoreType.DMA((slots,)),
+            pltpu.SemaphoreType.DMA((4,)),
         ],
     )(vort_div.reshape(4 * slots * degrees // 128, 128), legendre, owner, thickness.reshape(1, 1))
     totals = lax.all_to_all(
-        message.reshape(levels, 1, slots * 128), "lev", split_axis=0, concat_axis=0, tiled=True
-    ).reshape(levels * slots, 128)
-    table_high, table_low, phase_cos, phase_sin = call(
+        message.reshape(depth, 1, slots * 128),
+        "lev",
+        split_axis=0,
+        concat_axis=0,
+        tiled=True,
+        axis_index_groups=columns,
+    ).reshape(depth * slots, 128)
+    table_high, table_low, phase_cos, phase_sin, factors = call(
         table_kernel,
         name="tables",
-        in_specs=[vmem],
-        out_specs=(vmem, vmem, vmem, vmem),
+        in_specs=[vmem, smem, smem, smem],
+        out_specs=(vmem, vmem, vmem, vmem, vmem),
         out_shape=(
             shaped((waves * slots, 256), bf16),
             shaped((waves * slots, 256), bf16),
             shaped((slots // 2 * 16, 128)),
             shaped((slots // 2 * 16, 128)),
+            shaped((24, 128)),
         ),
-    )(local(owner_map.reshape(waves, slots)))
+    )(local(owner_map.reshape(waves, slots)), lat_sine, quad_weight, thickness)
     sent = call(
         prefix_kernel,
         name="prefix",
-        in_specs=[vmem, vmem, smem],
+        in_specs=[vmem, vmem] + [smem] * len(level),
         out_specs=vmem,
-        out_shape=shaped((rows, 128)),
-        scratch_shapes=[pltpu.VMEM((128, 128), f32)],
-    )(local(totals), local(fourier), level)
+        out_shape=shaped((2 * rows, 128)),
+        scratch_shapes=[pltpu.VMEM((256, 128), f32)],
+    )(local(totals), local(fourier), *level)
     got = lax.all_to_all(
-        sent.reshape(rows, 1, 128), "wave", split_axis=0, concat_axis=0, tiled=True
-    ).reshape(waves, 128)
+        sent.reshape(2 * rows, 1, 128),
+        ("wave", "lev"),
+        split_axis=0,
+        concat_axis=0,
+        tiled=True,
+        axis_index_groups=planes,
+    ).reshape(2 * waves, 128)
     flat = lambda x: local(x.reshape(count * length // 128, 128))
     spectra = call(
         grid_kernel,
         name="grid",
-        in_specs=[vmem] * 8 + [smem] * 3,
+        in_specs=[vmem] * 9,
         out_specs=vmem,
         out_shape=shaped((waves * 4, 128)),
     )(
@@ -431,9 +467,7 @@
         flat(tracers),
         flat(above),
         flat(below),
-        lat_sine,
-        quad_weight,
-        thickness,
+        local(factors),
     )
     back = lax.all_to_all(
         spectra.reshape(waves, 4, 128), "wave", split_axis=0, concat_axis=0, tiled=True

time: 87.8 us -> 80.6 us (0.918)
  blocking collectives: 20.8 us -> 43.9 us
  starting transfers between devices: 42.9 us -> 21.3 us
  waiting for transfers between devices: 13.6 us -> 6.73 us
  Pallas kernels: 7.86 us -> 6.04 us
    all_to_all x0 -> x1, blocking collectives: none -> 23.2 us  [shards(): lax.all_to_all(message.reshape(depth, 1, slots * 128), 'lev', split_axis=...]
    all_to_all x2 -> x1, starting transfers between devices: 33.6 us -> 15.1 us  [shards(): lax.all_to_all(sent.reshape(2 * rows, 1, 128), ('wave', 'lev'), split_axi...]
    all_to_all x2 -> x1, waiting for transfers between devices: 6.92 us -> 0.01 us  [shards(): lax.all_to_all(sent.reshape(2 * rows, 1, 128), ('wave', 'lev'), split_axi...]
    ppermute x1, starting transfers between devices: 7.45 us -> 4.23 us  [shards(): below = lax.ppermute(tracers, 'lev', down)]
    pallas_call x1, Pallas kernels: 4.02 us -> 2.2 us  [shards(): call(winds_kernel, name='winds', in_specs=[hbm, hbm, hbm, hbm], out_specs...]
  transfers between devices with their start and end apart: 4 -> 3, of which waited for: 2 -> 1; matrix products, arithmetic and copies ran while one was open for 0% -> 0% of each run, Pallas kernels for 1% -> 1%
where the time goes in v3:
time: 80.6 us; the launch traced here: 80.2 us
  blocking collectives  43.9 us (54%)
  starting transfers between devices  21.3 us (26%)
  waiting for transfers between devices  6.73 us (8%)
  Pallas kernels  6.04 us (7%)
  between operations  2.06 us (3%)
    all_to_all x1, blocking collectives, shards(): lax.all_to_all(message.reshape(depth, 1, slots * 128), 'lev', split_axis=...  23.2 us
    all_to_all x1, blocking collectives, shards(): lax.all_to_all(spectra.reshape(waves, 4, 128), 'wave', split_axis=0, conc...  20.8 us
    all_to_all x1, starting transfers between devices, shards(): lax.all_to_all(sent.reshape(2 * rows, 1, 128), ('wave', 'lev'), split_axi...  15.1 us
    ppermute x1, waiting for transfers between devices, shards(): above = lax.ppermute(tracers, 'lev', up)  6.72 us
    ppermute x1, starting transfers between devices, shards(): below = lax.ppermute(tracers, 'lev', down)  4.23 us
    pallas_call x1, Pallas kernels, shards(): call(winds_kernel, name='winds', in_specs=[hbm, hbm, hbm, hbm], out_specs...  2.2 us
    ppermute x1, starting transfers between devices, shards(): above = lax.ppermute(tracers, 'lev', up)  1.92 us
  transfers between devices with their start and end apart: 3, of which 1 were waited for; matrix products, arithmetic and copies ran while one was open for 0% of the time, Pallas kernels for 1%

profile of v3, /device:TPU:113, one launch (start us, length us, event | category | flops | bytes accessed | tf_op | source)
XLA Modules:
  0.0 80.2 jit_solution(16040522467950377823)
XLA Ops:
  0.0 0.0 copy-start.1
  0.0 0.0 copy-start
  0.7 2.2 %winds.1 = (f32[40,128]{1,0:T(8,128)S(1)}, f32[80,128]{1,0:T(8,128)S(1)}, bf16[640,640]{1,0:T(8,128)(2,1)S(1)}, bf16[640,640]{1,0:T(8,128)(2,1)S(1)}) custom-call(f32[200,128]{1,0:T(8,128)} %bitcast.23, f32[10,64,640]{2,1,0:T(8,128)} %leg_hbm.1, s32[640]{0:T(1024)} %owner_hbm.1, f32[1,1]{1,0:T(1,128)} %bitcast.14.thick_hbm), custom_call_target="tpu_custom_call" | custom-call | tf_op jit(solution)/shard_map/winds/pallas_call | solution.py:396
  2.9 23.2 %all_to_all.15 = f32[8,1,1280]{2,1,0:T(1,128)S(1)} all-to-all(f32[8,1,1280]{2,1,0:T(1,128)S(1)} %bitcast.22), channel_id=1, replica_groups={{0,1,2,3,4,5,6,7},{8,9,10,11,12,13,14,15},{16,17,18,19,20,21,22,23},{24..., dimensions={0} | all-to-all | bytes 81920 | tf_op jit(solution)/shard_map/all_to_all | solution.py:417
  26.1 0.8 %prefix.1 = f32[128,128]{1,0:T(8,128)} custom-call(f32[80,128]{1,0:T(8,128)S(1)} %bitcast.18, f32[40,128]{1,0:T(8,128)S(1)} %get-tuple-element.15.f_ref), custom_call_target="tpu_custom_call" | custom-call | tf_op jit(solution)/shard_map/prefix/pallas_call | solution.py:438
  26.9 15.1 %all-to-all-start.1 = ((f32[128,1,128]{2,1,0:T(1,128)}), f32[128,1,128]{2,1,0:T(1,128)S(1)}, u32[]{:S(2)}, u32[]{:S(2)}) async-start(f32[128,1,128]{2,1,0:T(1,128)} %bitcast.5), calls=%async_computation.1 | async-start | bytes 131072 | tf_op jit(solution)/shard_map/all_to_all | solution.py:446
  42.0 0.0 copy-done
  42.1 4.2 %collective-permute-start.1 = (f32[8,1,1,1280]{3,2,1,0:T(1,128)S(1)}, f32[8,1,1,1280]{3,2,1,0:T(1,128)S(1)}, u32[]{:S(2)}, u32[]{:S(2)}) collective-permute-start(f32[8,1,1,1280]{3,2,1,0:T(1,128)S(1)} %copy-done), channel_id=1, source_target_pairs={{1,0},{2,1},{3,2},{4,3},{5,4},{6,5},{7,6},{8,7},{9,8},{10,9},{11,1... | collective-permute-start | bytes 122888 | tf_op jit(solution)/shard_map/ppermute | solution.py:386
  46.3 1.9 %collective-permute-start = (f32[8,1,1,1280]{3,2,1,0:T(1,128)S(1)}, f32[8,1,1,1280]{3,2,1,0:T(1,128)S(1)}, u32[]{:S(2)}, u32[]{:S(2)}) collective-permute-start(f32[8,1,1,1280]{3,2,1,0:T(1,128)S(1)} %copy-done), channel_id=1, source_target_pairs={{0,1},{1,2},{2,3},{3,4},{4,5},{5,6},{6,7},{7,8},{8,9},{9,10},{10,1... | collective-permute-start | bytes 122888 | tf_op jit(solution)/shard_map/ppermute | solution.py:385
  48.2 0.0 copy-done.1
  48.2 0.1 reshape.45.owner_ref
  49.7 0.7 tables.1
  50.3 0.0 collective-permute-done.1
  50.3 6.7 %collective-permute-done = f32[8,1,1,1280]{3,2,1,0:T(1,128)S(1)} collective-permute-done((f32[8,1,1,1280]{3,2,1,0:T(1,128)S(1)}, f32[8,1,1,1280]{3,2,1,0:T(1,128)S(1)}, u32[]{:S(2)}, u32[]{:S(2)}) %collective-permute-start) | collective-permute-done | bytes 40992 | tf_op jit(solution)/shard_map/ppermute | solution.py:385
  57.1 0.0 all-to-all-done.1
  57.1 1.1 %grid.1 = f32[256,128]{1,0:T(8,128)S(1)} custom-call(f32[128,128]{1,0:T(8,128)S(1)} %bitcast.17, bf16[640,256]{1,0:T(8,128)(2,1)S(1)} %get-tuple-element.16.table_high_ref, bf16[640,256]{1,0:T(8,128)(2,1)S(1)} %get-tuple-element.17.table_low_ref, f32[80,128]{1,0:T(8,128)S(1)} %get-tuple-element.18.phase_cos_ref, ...), custom_call_target="tpu_custom_call" | custom-call | tf_op jit(solution)/shard_map/grid/pallas_call | solution.py:455
  58.2 20.8 %all_to_all.16 = f32[64,4,128]{2,1,0:T(4,128)S(1)} all-to-all(f32[64,4,128]{2,1,0:T(4,128)S(1)} %bitcast.16), channel_id=1, replica_groups=mesh['wave'=64,'lev'=16] {'wave'}, dimensions={0} | all-to-all | bytes 262144 | tf_op jit(solution)/shard_map/all_to_all | solution.py:472
  79.0 1.3 %result.1 = f32[800,128]{1,0:T(8,128)} custom-call(f32[256,128]{1,0:T(8,128)S(1)} %bitcast.15, bf16[640,640]{1,0:T(8,128)(2,1)S(1)} %get-tuple-element.21.high_ref, bf16[640,640]{1,0:T(8,128)(2,1)S(1)} %get-tuple-element.22.low_ref), custom_call_target="tpu_custom_call" | custom-call | tf_op jit(solution)/shard_map/result/pallas_call | solution.py:475
Async XLA Ops:
  0.0 48.2 %copy-start.1 = (s32[640]{0:T(1024)S(1)}, s32[640]{0:T(1024)}, u32[]{:S(2)}) copy-start(s32[640]{0:T(1024)} %owner_hbm.1) | copy-start | bytes 7684
  0.0 42.0 %copy-start = (f32[8,1,1,1280]{3,2,1,0:T(1,128)S(1)}, f32[8,1,1,1280]{3,2,1,0:T(1,128)}, u32[]{:S(2)}) copy-start(f32[8,1,1,1280]{3,2,1,0:T(1,128)} %param.13) | copy-start | bytes 122884
  26.9 30.2 %all-to-all-start.1 = ((f32[128,1,128]{2,1,0:T(1,128)}), f32[128,1,128]{2,1,0:T(1,128)S(1)}, u32[]{:S(2)}, u32[]{:S(2)}) async-start(f32[128,1,128]{2,1,0:T(1,128)} %bitcast.5), calls=%async_computation.1 | async-start | bytes 131072 | tf_op jit(solution)/shard_map/all_to_all | solution.py:446
  42.1 8.3 %collective-permute-start.1 = (f32[8,1,1,1280]{3,2,1,0:T(1,128)S(1)}, f32[8,1,1,1280]{3,2,1,0:T(1,128)S(1)}, u32[]{:S(2)}, u32[]{:S(2)}) collective-permute-start(f32[8,1,1,1280]{3,2,1,0:T(1,128)S(1)} %copy-done), channel_id=1, source_target_pairs={{1,0},{2,1},{3,2},{4,3},{5,4},{6,5},{7,6},{8,7},{9,8},{10,9},{11,1... | collective-permute-start | bytes 122888 | tf_op jit(solution)/shard_map/ppermute | solution.py:386
  46.3 10.8 %collective-permute-start = (f32[8,1,1,1280]{3,2,1,0:T(1,128)S(1)}, f32[8,1,1,1280]{3,2,1,0:T(1,128)S(1)}, u32[]{:S(2)}, u32[]{:S(2)}) collective-permute-start(f32[8,1,1,1280]{3,2,1,0:T(1,128)S(1)} %copy-done), channel_id=1, source_target_pairs={{0,1},{1,2},{2,3},{3,4},{4,5},{5,6},{6,7},{7,8},{8,9},{9,10},{10,1... | collective-permute-start | bytes 122888 | tf_op jit(solution)/shard_map/ppermute | solution.py:385

commit v4 on v2

--- a/solution.py
+++ b/solution.py
@@ -1,3 +1,4 @@
+import functools
 import math
 
 import jax
@@ -78,7 +79,6 @@
     field_ref,
     msg_ref,
     sem,
-    leg_sem,
 ):
     slots, rows, degrees = leg_ref.shape
     copies = lev_ref.shape[0] // slots
@@ -90,10 +90,8 @@
     thick_copy.start(priority=1)
     vort_copy.start(priority=1)
 
-    def leg_copy(s):
-        return pltpu.make_async_copy(leg_hbm.at[s], leg_ref.at[s], leg_sem.at[s])
-
-    lax.fori_loop(0, slots, lambda s, _: leg_copy(s).start(), None)
+    leg_copy = pltpu.make_async_copy(leg_hbm, leg_ref, sem.at[3])
+    leg_copy.start()
     owner_copy.wait()
     own = own_orders(owner_ref, slots)
     row = lax.broadcasted_iota(jnp.int32, (slots, degrees), 0)
@@ -130,6 +128,7 @@
 
     vort_copy.wait()
     thick_copy.wait()
+    leg_copy.wait()
     div_real = vort(2)
     div_imag = vort(3)
     stream_real = inverse * vort(0)
@@ -171,7 +170,6 @@
         highs, lows = [], []
         for parity in range(2):
             s = 2 * t + parity
-            leg_copy(s).wait()
             leg_high, leg_low = halves(jnp.where(valid[s : s + 1], leg_ref[s], 0.0))
             high_ref[s * rows : (s + 1) * rows, :] = leg_high
             low_ref[s * rows : (s + 1) * rows, :] = leg_low
@@ -188,9 +186,27 @@
         lev_ref[copy * slots : (copy + 1) * slots, :] = message
 
 
-def table_kernel(owner_ref, table_high_ref, table_low_ref, phase_cos_ref, phase_sin_ref):
+def table_kernel(
+    owner_ref,
+    sine_hbm,
+    weight_hbm,
+    thick_hbm,
+    table_high_ref,
+    table_low_ref,
+    phase_cos_ref,
+    phase_sin_ref,
+    factor_ref,
+    scalar_ref,
+    sem,
+):
     waves, slots = owner_ref.shape
     length = 2.0 * waves * slots
+    copies = [
+        pltpu.make_async_copy(source, scalar_ref.at[pl.ds(i, 1)], sem.at[i])
+        for i, source in enumerate((sine_hbm, weight_hbm, thick_hbm))
+    ]
+    for copy in copies:
+        copy.start()
     orders = owner_ref[...].astype(f32)
     offset = lax.broadcasted_iota(jnp.int32, (waves, 128), 1).astype(f32)
     padded = jnp.concatenate([orders, jnp.zeros((waves, 128 - slots), f32)], axis=1)
@@ -211,14 +227,23 @@
         cosine, sine = cos_sin(row * block * 128.0, length / 4.0)
         phase_cos_ref[t * blocks : (t + 1) * blocks, :] = cosine
         phase_sin_ref[t * blocks : (t + 1) * blocks, :] = sine
-
-
-def prefix_kernel(got_ref, f_ref, level_ref, out_ref, ft_ref):
+    for copy in copies:
+        copy.wait()
+    step = 2.0 * math.pi / length
+    sine = scalar_ref[0, 0]
+    weight = jnp.full((8, 128), -scalar_ref[1, 0] * (2.0 / length), f32)
+    slope = weight / ((1.0 - sine * sine) * (2.0 * step))
+    factor_ref[0:8, :] = slope
+    factor_ref[8:16, :] = slope
+    factor_ref[16:24, :] = weight / (2.0 * scalar_ref[2, 0])
+
+
+def prefix_kernel(got_ref, f_ref, *rest):
+    level_ref, out_ref, ft_ref = rest if INTERPRET else (None, *rest)
+    level = level_ref[0] if INTERPRET else lax.axis_index("lev")
     pairs = f_ref.shape[0] // 8
-    copies = got_ref.shape[0] // (2 * pairs)
-    level = level_ref[0]
     total = jnp.zeros((2 * pairs, 128), f32)
-    for source in range(copies):
+    for source in range(got_ref.shape[0] // (2 * pairs)):
         part = got_ref[source * 2 * pairs : (source + 1) * 2 * pairs, :]
         total = total + jnp.where(source < level, part, 0.0)
     ft_ref[0 : 8 * pairs, :] = f_ref[...]
@@ -239,11 +264,15 @@
     q_ref,
     above_ref,
     below_ref,
-    sine_ref,
-    weight_ref,
-    thick_ref,
-    out_ref,
+    cross_ref,
+    factor_ref,
+    *rest,
+    depth,
 ):
+    level_ref, out_ref = rest if INTERPRET else (None, *rest)
+    level = level_ref[0] if INTERPRET else lax.axis_index("lev")
+    first_level = level % depth == 0
+    last_level = level % depth == depth - 1
     waves = got_ref.shape[0]
     pairs = 5
     blocks = phase_cos_ref.shape[0] // pairs
@@ -267,21 +296,18 @@
     table_high = table_high_ref[...]
     table_low = table_low_ref[...]
     grid = three_products(turned, table_high, table_low, dot_nn)
-    length = 128.0 * used
-    lon_step = 2.0 * math.pi / length
-    lat_step = 2.0 * math.pi / length
-    sine = sine_ref[0]
-    metric = 1.0 - sine * sine
-    weight = -weight_ref[0] * (2.0 / length)
-    zonal_factor = weight / (metric * (2.0 * lon_step))
-    merid_factor = weight / (metric * (2.0 * lat_step))
-    vertical_factor = weight / (2.0 * thick_ref[0])
+    zonal_factor = factor_ref[0:8, :]
+    merid_factor = factor_ref[8:16, :]
+    vertical_factor = factor_ref[16:24, :]
     lane = lax.broadcasted_iota(jnp.int32, (8, 128), 1)
     east, other, merid = [], [], []
     for b in range(used):
         q = q_ref[pl.ds(b, 8, stride=used), :]
         above = above_ref[pl.ds(b, 8, stride=used), :]
         below = below_ref[pl.ds(b, 8, stride=used), :]
+        cross = cross_ref[pl.ds(b, 8, stride=used), :]
+        above = jnp.where(first_level, cross, above)
+        below = jnp.where(last_level, cross, below)
         field = grid[8 * b : 8 * b + 4, 0:128] + grid[8 * b + 4 : 8 * b + 8, 128:256]
         east.append(field[0:1] * q)
         merid.append(field[1:2] * q)
@@ -308,7 +334,7 @@
                 cos_total = cos_total + phase_cos[b][t] * c + phase_sin[b][t] * s
                 sin_total = sin_total + phase_cos[b][t] * s - phase_sin[b][t] * c
             stack += [cos_total, sin_total]
-        stack.append(jnp.full((128 - 16 * pairs, 128), merid_factor, f32))
+        stack += [merid_factor] * (16 - 2 * pairs)
         sent = jnp.concatenate(stack, axis=0).T
         for parity in range(2):
             out_ref[pl.ds(kind * 2 + parity, waves, stride=4), :] = sent[parity * 64 : parity * 64 + waves]
@@ -359,14 +385,18 @@
     levels = lax.axis_size("lev")
     count, _, _, length = tracers.shape
     call = lambda kernel, **kw: pl.pallas_call(kernel, interpret=INTERPRET, **kw)
-    up = [(i, i + 1) for i in range(levels - 1)]
+    depth = levels // 2
+    starts = [half * depth for half in range(2)]
+    up = [(h + z, h + (z + 1) % depth) for h in starts for z in range(depth)]
     down = [(b, a) for a, b in up]
     above = lax.ppermute(tracers, "lev", up)
     below = lax.ppermute(tracers, "lev", down)
+    around = jnp.where(lax.axis_index("lev") % depth == 0, above, below)
+    cross = lax.ppermute(around, "lev", [(0, depth), (levels - 1, depth - 1)])
     owner = owner_map
     if INTERPRET:
         owner = jnp.concatenate([owner_map, lax.axis_index("wave").reshape(1)])
-    level = lax.axis_index("lev").astype(jnp.int32).reshape(1)
+    level = (lax.axis_index("lev").reshape(1),) if INTERPRET else ()
     fourier, message, leg_high, leg_low = call(
         winds_kernel,
         name="winds",
@@ -385,41 +415,42 @@
             pltpu.SMEM((1, 1), f32),
             pltpu.VMEM((degrees, 128), f32),
             pltpu.VMEM((slots, 128), f32),
-            pltpu.SemaphoreType.DMA((3,)),
-            pltpu.SemaphoreType.DMA((slots,)),
+            pltpu.SemaphoreType.DMA((4,)),
         ],
     )(vort_div.reshape(4 * slots * degrees // 128, 128), legendre, owner, thickness.reshape(1, 1))
     totals = lax.all_to_all(
         message.reshape(levels, 1, slots * 128), "lev", split_axis=0, concat_axis=0, tiled=True
     ).reshape(levels * slots, 128)
-    table_high, table_low, phase_cos, phase_sin = call(
+    table_high, table_low, phase_cos, phase_sin, factors = call(
         table_kernel,
         name="tables",
-        in_specs=[vmem],
-        out_specs=(vmem, vmem, vmem, vmem),
+        in_specs=[vmem, hbm, hbm, hbm],
+        out_specs=(vmem, vmem, vmem, vmem, vmem),
+        scratch_shapes=[pltpu.SMEM((3, 1), f32), pltpu.SemaphoreType.DMA((3,))],
         out_shape=(
             shaped((waves * slots, 256), bf16),
             shaped((waves * slots, 256), bf16),
             shaped((slots // 2 * 16, 128)),
             shaped((slots // 2 * 16, 128)),
+            shaped((24, 128)),
         ),
-    )(local(owner_map.reshape(waves, slots)))
+    )(local(owner_map.reshape(waves, slots)), *(x.reshape(1, 1) for x in (lat_sine, quad_weight, thickness)))
     sent = call(
         prefix_kernel,
         name="prefix",
-        in_specs=[vmem, vmem, smem],
+        in_specs=[vmem, vmem] + [smem] * len(level),
         out_specs=vmem,
         out_shape=shaped((rows, 128)),
         scratch_shapes=[pltpu.VMEM((128, 128), f32)],
-    )(local(totals), local(fourier), level)
+    )(local(totals), local(fourier), *level)
     got = lax.all_to_all(
         sent.reshape(rows, 1, 128), "wave", split_axis=0, concat_axis=0, tiled=True
     ).reshape(waves, 128)
     flat = lambda x: local(x.reshape(count * length // 128, 128))
     spectra = call(
-        grid_kernel,
+        functools.partial(grid_kernel, depth=depth),
         name="grid",
-        in_specs=[vmem] * 8 + [smem] * 3,
+        in_specs=[vmem] * 10 + [smem] * len(level),
         out_specs=vmem,
         out_shape=shaped((waves * 4, 128)),
     )(
@@ -431,9 +462,9 @@
         flat(tracers),
         flat(above),
         flat(below),
-        lat_sine,
-        quad_weight,
-        thickness,
+        flat(cross),
+        local(factors),
+        *level,
     )
     back = lax.all_to_all(
         spectra.reshape(waves, 4, 128), "wave", split_axis=0, concat_axis=0, tiled=True

time: 87.8 us -> 77.6 us (0.88)
  waiting for transfers between devices: 13.6 us -> 5.17 us
  starting transfers between devices: 42.9 us -> 41.3 us
    ppermute x1, waiting for transfers between devices: 6.72 us -> 0.01 us  [shards(): above = lax.ppermute(tracers, 'lev', up)]
    all_to_all x1, waiting for transfers between devices: 6.92 us -> 0.39 us  [shards(): lax.all_to_all(message.reshape(levels, 1, slots * 128), 'lev', split_axis...]
    ppermute x0 -> x1, waiting for transfers between devices: none -> 4.77 us  [shards(): cross = lax.ppermute(around, 'lev', [(0, depth), (levels - 1, depth - 1)])]
    ppermute x1, starting transfers between devices: 7.45 us -> 3.4 us  [shards(): below = lax.ppermute(tracers, 'lev', down)]
    ppermute x0 -> x1, starting transfers between devices: none -> 1.29 us  [shards(): cross = lax.ppermute(around, 'lev', [(0, depth), (levels - 1, depth - 1)])]
    pallas_call x1, Pallas kernels: 4.02 us -> 2.84 us  [shards(): call(winds_kernel, name='winds', in_specs=[hbm, hbm, hbm, hbm], out_specs...]
    ppermute x1, starting transfers between devices: 1.92 us -> 3.09 us  [shards(): above = lax.ppermute(tracers, 'lev', up)]
  transfers between devices with their start and end apart: 4 -> 5, of which waited for: 2 -> 2; matrix products, arithmetic and copies ran while one was open for 0% -> 0% of each run, Pallas kernels for 1% -> 3%
where the time goes in v4:
time: 77.6 us; the launch traced here: 76.4 us
  starting transfers between devices  41.3 us (53%)
  blocking collectives  20.4 us (26%)
  Pallas kernels  7.25 us (9%)
  waiting for transfers between devices  5.17 us (7%)
  between operations  2.09 us (3%)
    all_to_all x1, starting transfers between devices, shards(): lax.all_to_all(message.reshape(levels, 1, slots * 128), 'lev', split_axis...  21.5 us
    all_to_all x1, blocking collectives, shards(): lax.all_to_all(spectra.reshape(waves, 4, 128), 'wave', split_axis=0, conc...  20.4 us
    all_to_all x1, starting transfers between devices, shards(): lax.all_to_all(sent.reshape(rows, 1, 128), 'wave', split_axis=0, concat_a...  12 us
    ppermute x1, waiting for transfers between devices, shards(): cross = lax.ppermute(around, 'lev', [(0, depth), (levels - 1, depth - 1)])  4.77 us
    ppermute x1, starting transfers between devices, shards(): below = lax.ppermute(tracers, 'lev', down)  3.4 us
    ppermute x1, starting transfers between devices, shards(): above = lax.ppermute(tracers, 'lev', up)  3.09 us
    pallas_call x1, Pallas kernels, shards(): call(winds_kernel, name='winds', in_specs=[hbm, hbm, hbm, hbm], out_specs...  2.84 us
  transfers between devices with their start and end apart: 5, of which 2 were waited for; matrix products, arithmetic and copies ran while one was open for 0% of the time, Pallas kernels for 3%

profile of v4, /device:TPU:113, one launch (start us, length us, event | category | flops | bytes accessed | tf_op | source)
XLA Modules:
  0.0 76.4 jit_solution(7671263594174863860)
XLA Ops:
  0.0 0.0 copy-start.1
  0.0 0.0 copy-start
  0.7 2.8 %winds.1 = (f32[40,128]{1,0:T(8,128)S(1)}, f32[160,128]{1,0:T(8,128)}, bf16[640,640]{1,0:T(8,128)(2,1)S(1)}, bf16[640,640]{1,0:T(8,128)(2,1)S(1)}) custom-call(f32[200,128]{1,0:T(8,128)} %bitcast.29, f32[10,64,640]{2,1,0:T(8,128)} %leg_hbm.1, s32[640]{0:T(1024)} %owner_hbm.1, f32[1,1]{1,0:T(1,128)} %bitcast.19.thick_hbm), custom_call_target="tpu_custom_call" | custom-call | tf_op jit(solution)/shard_map/winds/pallas_call | solution.py:400
  3.5 21.5 %all-to-all-start = ((f32[16,1,1280]{2,1,0:T(1,128)}), f32[16,1,1280]{2,1,0:T(1,128)S(1)}, u32[]{:S(2)}, u32[]{:S(2)}) async-start(f32[16,1,1280]{2,1,0:T(1,128)} %bitcast.2), calls=%async_computation | async-start | bytes 163840 | tf_op jit(solution)/shard_map/all_to_all | solution.py:421
  25.0 0.0 copy-done
  25.1 3.1 %collective-permute-start = (f32[8,1,1,1280]{3,2,1,0:T(1,128)S(1)}, f32[8,1,1,1280]{3,2,1,0:T(1,128)S(1)}, u32[]{:S(2)}, u32[]{:S(2)}) collective-permute-start(f32[8,1,1,1280]{3,2,1,0:T(1,128)S(1)} %copy-done), channel_id=1, source_target_pairs={{0,1},{1,2},{2,3},{3,4},{4,5},{5,6},{6,7},{7,0},{8,9},{9,10},{10,1... | collective-permute-start | bytes 122888 | tf_op jit(solution)/shard_map/ppermute | solution.py:392
  28.2 3.4 %collective-permute-start.1 = (f32[8,1,1,1280]{3,2,1,0:T(1,128)S(1)}, f32[8,1,1,1280]{3,2,1,0:T(1,128)S(1)}, u32[]{:S(2)}, u32[]{:S(2)}) collective-permute-start(f32[8,1,1,1280]{3,2,1,0:T(1,128)S(1)} %copy-done), channel_id=1, source_target_pairs={{1,0},{2,1},{3,2},{4,3},{5,4},{6,5},{7,6},{0,7},{9,8},{10,9},{11,1... | collective-permute-start | bytes 122888 | tf_op jit(solution)/shard_map/ppermute | solution.py:393
  31.6 0.4 all-to-all-done
  32.0 0.8 %prefix.1 = f32[64,128]{1,0:T(8,128)} custom-call(f32[160,128]{1,0:T(8,128)S(1)} %bitcast.23, f32[40,128]{1,0:T(8,128)S(1)} %get-tuple-element.15.f_ref), custom_call_target="tpu_custom_call" | custom-call | tf_op jit(solution)/shard_map/prefix/pallas_call | solution.py:438
  32.8 12.0 %all-to-all-start.1 = ((f32[64,1,128]{2,1,0:T(1,128)}), f32[64,1,128]{2,1,0:T(1,128)S(1)}, u32[]{:S(2)}, u32[]{:S(2)}) async-start(f32[64,1,128]{2,1,0:T(1,128)} %bitcast.5), calls=%async_computation.1 | async-start | bytes 65536 | tf_op jit(solution)/shard_map/all_to_all | solution.py:446
  44.8 0.0 collective-permute-done
  44.8 0.0 collective-permute-done.1
  44.9 1.3 %collective-permute-start.2 = (f32[8,1,1,1280]{3,2,1,0:T(1,128)S(1)}, f32[8,1,1,1280]{3,2,1,0:T(1,128)S(1)}, u32[]{:S(2)}, u32[]{:S(2)}) collective-permute-start(f32[8,1,1,1280]{3,2,1,0:T(1,128)S(1)} %broadcast_select_fusion), channel_id=1, source_target_pairs={{0,8},{15,7},{16,24},{31,23},{32,40},{47,39},{48,56},{63,55},{64,7... | collective-permute-start | bytes 122888 | tf_op jit(solution)/shard_map/ppermute | solution.py:395
  46.2 0.0 copy-done.1
  46.2 0.1 reshape.55.owner_ref
  47.6 1.2 %tables.1 = (bf16[640,256]{1,0:T(8,128)(2,1)S(1)}, bf16[640,256]{1,0:T(8,128)(2,1)S(1)}, f32[80,128]{1,0:T(8,128)S(1)}, f32[80,128]{1,0:T(8,128)S(1)}, f32[24,128]{1,0:T(8,128)S(1)}) custom-call(s32[64,10]{1,0:T(8,128)S(1)} %reshape.55.owner_ref, f32[1,1]{1,0:T(1,128)} %bitcast.17.sine_hbm, f32[1,1]{1,0:T(1,128)} %bitcast.18.weight_hbm, ...), custom_call_target="tpu_custom_call" | custom-call | tf_op jit(solution)/shard_map/tables/pallas_call | solution.py:424
  48.9 4.8 %collective-permute-done.2 = f32[8,1,1,1280]{3,2,1,0:T(1,128)S(1)} collective-permute-done((f32[8,1,1,1280]{3,2,1,0:T(1,128)S(1)}, f32[8,1,1,1280]{3,2,1,0:T(1,128)S(1)}, u32[]{:S(2)}, u32[]{:S(2)}) %collective-permute-start.2) | collective-permute-done | bytes 40992 | tf_op jit(solution)/shard_map/ppermute | solution.py:395
  53.6 0.0 all-to-all-done.1
  53.7 1.1 %grid.1 = f32[256,128]{1,0:T(8,128)S(1)} custom-call(f32[64,128]{1,0:T(8,128)S(1)} %bitcast.26, bf16[640,256]{1,0:T(8,128)(2,1)S(1)} %get-tuple-element.16.table_high_ref, bf16[640,256]{1,0:T(8,128)(2,1)S(1)} %get-tuple-element.17.table_low_ref, f32[80,128]{1,0:T(8,128)S(1)} %get-tuple-element.18.phase_cos_ref, ...), custom_call_target="tpu_custom_call" | custom-call | tf_op jit(solution)/shard_map/grid/pallas_call | solution.py:450
  54.8 20.4 %all_to_all.15 = f32[64,4,128]{2,1,0:T(4,128)S(1)} all-to-all(f32[64,4,128]{2,1,0:T(4,128)S(1)} %bitcast.21), channel_id=1, replica_groups=mesh['wave'=64,'lev'=16] {'wave'}, dimensions={0} | all-to-all | bytes 262144 | tf_op jit(solution)/shard_map/all_to_all | solution.py:469
  75.2 1.3 %result.1 = f32[800,128]{1,0:T(8,128)} custom-call(f32[256,128]{1,0:T(8,128)S(1)} %bitcast.22, bf16[640,640]{1,0:T(8,128)(2,1)S(1)} %get-tuple-element.21.high_ref, bf16[640,640]{1,0:T(8,128)(2,1)S(1)} %get-tuple-element.22.low_ref), custom_call_target="tpu_custom_call" | custom-call | tf_op jit(solution)/shard_map/result/pallas_call | solution.py:472
  (1 shorter events, 0.0 us)
Async XLA Ops:
  0.0 46.2 %copy-start.1 = (s32[640]{0:T(1024)S(1)}, s32[640]{0:T(1024)}, u32[]{:S(2)}) copy-start(s32[640]{0:T(1024)} %owner_hbm.1) | copy-start | bytes 7684
  0.0 25.0 %copy-start = (f32[8,1,1,1280]{3,2,1,0:T(1,128)S(1)}, f32[8,1,1,1280]{3,2,1,0:T(1,128)}, u32[]{:S(2)}) copy-start(f32[8,1,1,1280]{3,2,1,0:T(1,128)} %param.13) | copy-start | bytes 122884
  3.5 28.4 %all-to-all-start = ((f32[16,1,1280]{2,1,0:T(1,128)}), f32[16,1,1280]{2,1,0:T(1,128)S(1)}, u32[]{:S(2)}, u32[]{:S(2)}) async-start(f32[16,1,1280]{2,1,0:T(1,128)} %bitcast.2), calls=%async_computation | async-start | bytes 163840 | tf_op jit(solution)/shard_map/all_to_all | solution.py:421
  25.1 19.8 %collective-permute-start = (f32[8,1,1,1280]{3,2,1,0:T(1,128)S(1)}, f32[8,1,1,1280]{3,2,1,0:T(1,128)S(1)}, u32[]{:S(2)}, u32[]{:S(2)}) collective-permute-start(f32[8,1,1,1280]{3,2,1,0:T(1,128)S(1)} %copy-done), channel_id=1, source_target_pairs={{0,1},{1,2},{2,3},{3,4},{4,5},{5,6},{6,7},{7,0},{8,9},{9,10},{10,1... | collective-permute-start | bytes 122888 | tf_op jit(solution)/shard_map/ppermute | solution.py:392
  28.2 16.7 %collective-permute-start.1 = (f32[8,1,1,1280]{3,2,1,0:T(1,128)S(1)}, f32[8,1,1,1280]{3,2,1,0:T(1,128)S(1)}, u32[]{:S(2)}, u32[]{:S(2)}) collective-permute-start(f32[8,1,1,1280]{3,2,1,0:T(1,128)S(1)} %copy-done), channel_id=1, source_target_pairs={{1,0},{2,1},{3,2},{4,3},{5,4},{6,5},{7,6},{0,7},{9,8},{10,9},{11,1... | collective-permute-start | bytes 122888 | tf_op jit(solution)/shard_map/ppermute | solution.py:393
  32.8 20.9 %all-to-all-start.1 = ((f32[64,1,128]{2,1,0:T(1,128)}), f32[64,1,128]{2,1,0:T(1,128)S(1)}, u32[]{:S(2)}, u32[]{:S(2)}) async-start(f32[64,1,128]{2,1,0:T(1,128)} %bitcast.5), calls=%async_computation.1 | async-start | bytes 65536 | tf_op jit(solution)/shard_map/all_to_all | solution.py:446
  44.9 8.8 %collective-permute-start.2 = (f32[8,1,1,1280]{3,2,1,0:T(1,128)S(1)}, f32[8,1,1,1280]{3,2,1,0:T(1,128)S(1)}, u32[]{:S(2)}, u32[]{:S(2)}) collective-permute-start(f32[8,1,1,1280]{3,2,1,0:T(1,128)S(1)} %broadcast_select_fusion), channel_id=1, source_target_pairs={{0,8},{15,7},{16,24},{31,23},{32,40},{47,39},{48,56},{63,55},{64,7... | collective-permute-start | bytes 122888 | tf_op jit(solution)/shard_map/ppermute | solution.py:395

commit v5 on v3

--- a/solution.py
+++ b/solution.py
@@ -269,8 +269,11 @@
     above_ref,
     below_ref,
     factor_ref,
-    out_ref,
+    *rest,
 ):
+    level_ref, out_ref = rest if INTERPRET else (None, *rest)
+    level = level_ref[0] if INTERPRET else lax.axis_index("lev")
+    even = level % 2 == 0
     waves = got_ref.shape[0] // 2
     pairs = 5
     blocks = phase_cos_ref.shape[0] // pairs
@@ -303,6 +306,7 @@
         q = q_ref[pl.ds(b, 8, stride=used), :]
         above = above_ref[pl.ds(b, 8, stride=used), :]
         below = below_ref[pl.ds(b, 8, stride=used), :]
+        above, below = jnp.where(even, above, below), jnp.where(even, below, above)
         field = grid[8 * b : 8 * b + 4, 0:128] + grid[8 * b + 4 : 8 * b + 8, 128:256]
         east.append(field[0:1] * q)
         merid.append(field[1:2] * q)
@@ -380,10 +384,10 @@
     levels = lax.axis_size("lev")
     count, _, _, length = tracers.shape
     call = lambda kernel, **kw: pl.pallas_call(kernel, interpret=INTERPRET, **kw)
-    up = [(i, i + 1) for i in range(levels - 1)]
-    down = [(b, a) for a, b in up]
-    above = lax.ppermute(tracers, "lev", up)
-    below = lax.ppermute(tracers, "lev", down)
+    swaps = []
+    for first in range(2):
+        pairs = [(i, i + 1) for i in range(first, levels - 1, 2)]
+        swaps.append(lax.ppermute(tracers, "lev", pairs + [(b, a) for a, b in pairs]))
     owner = owner_map
     if INTERPRET:
         owner = jnp.concatenate([owner_map, lax.axis_index("wave").reshape(1)])
@@ -455,7 +459,7 @@
     spectra = call(
         grid_kernel,
         name="grid",
-        in_specs=[vmem] * 9,
+        in_specs=[vmem] * 9 + [smem] * len(level),
         out_specs=vmem,
         out_shape=shaped((waves * 4, 128)),
     )(
@@ -465,9 +469,10 @@
         local(phase_cos),
         local(phase_sin),
         flat(tracers),
-        flat(above),
-        flat(below),
+        flat(swaps[1]),
+        flat(swaps[0]),
         local(factors),
+        *level,
     )
     back = lax.all_to_all(
         spectra.reshape(waves, 4, 128), "wave", split_axis=0, concat_axis=0, tiled=True

time: 80.6 us -> 78.8 us (0.978)
  waiting for transfers between devices: 6.73 us -> 4.36 us
    ppermute x2, waiting for transfers between devices: 6.72 us -> 4.36 us  [shards(): lax.ppermute(tracers, 'lev', pairs + [(b, a) for a, b in pairs])]
where the time goes in v5:
time: 78.8 us; the launch traced here: 78.4 us
  blocking collectives  44.1 us (56%)
  starting transfers between devices  21.7 us (28%)
  Pallas kernels  6.04 us (8%)
  waiting for transfers between devices  4.36 us (6%)
  between operations  2.06 us (3%)
    all_to_all x1, blocking collectives, shards(): lax.all_to_all(message.reshape(depth, 1, slots * 128), 'lev', split_axis=...  23.2 us
    all_to_all x1, blocking collectives, shards(): lax.all_to_all(spectra.reshape(waves, 4, 128), 'wave', split_axis=0, conc...  20.9 us
    all_to_all x1, starting transfers between devices, shards(): lax.all_to_all(sent.reshape(2 * rows, 1, 128), ('wave', 'lev'), split_axi...  15.1 us
    ppermute x2, starting transfers between devices, shards(): lax.ppermute(tracers, 'lev', pairs + [(b, a) for a, b in pairs])  6.58 us
    ppermute x2, waiting for transfers between devices, shards(): lax.ppermute(tracers, 'lev', pairs + [(b, a) for a, b in pairs])  4.36 us
    pallas_call x1, Pallas kernels, shards(): call(winds_kernel, name='winds', in_specs=[hbm, hbm, hbm, hbm], out_specs...  2.2 us
  transfers between devices with their start and end apart: 3, of which 1 were waited for; matrix products, arithmetic and copies ran while one was open for 0% of the time, Pallas kernels for 1%

profile of v5, /device:TPU:113, one launch (start us, length us, event | category | flops | bytes accessed | tf_op | source)
XLA Modules:
  0.0 78.4 jit_solution(6777497295419822610)
XLA Ops:
  0.0 0.0 copy-start.1
  0.0 0.0 copy-start
  0.7 2.2 %winds.1 = (f32[40,128]{1,0:T(8,128)S(1)}, f32[80,128]{1,0:T(8,128)S(1)}, bf16[640,640]{1,0:T(8,128)(2,1)S(1)}, bf16[640,640]{1,0:T(8,128)(2,1)S(1)}) custom-call(f32[200,128]{1,0:T(8,128)} %bitcast.23, f32[10,64,640]{2,1,0:T(8,128)} %leg_hbm.1, s32[640]{0:T(1024)} %owner_hbm.1, f32[1,1]{1,0:T(1,128)} %bitcast.14.thick_hbm), custom_call_target="tpu_custom_call" | custom-call | tf_op jit(solution)/shard_map/winds/pallas_call | solution.py:400
  2.9 23.2 %all_to_all.15 = f32[8,1,1280]{2,1,0:T(1,128)S(1)} all-to-all(f32[8,1,1280]{2,1,0:T(1,128)S(1)} %bitcast.22), channel_id=1, replica_groups={{0,1,2,3,4,5,6,7},{8,9,10,11,12,13,14,15},{16,17,18,19,20,21,22,23},{24..., dimensions={0} | all-to-all | bytes 81920 | tf_op jit(solution)/shard_map/all_to_all | solution.py:421
  26.1 0.8 %prefix.1 = f32[128,128]{1,0:T(8,128)} custom-call(f32[80,128]{1,0:T(8,128)S(1)} %bitcast.18, f32[40,128]{1,0:T(8,128)S(1)} %get-tuple-element.15.f_ref), custom_call_target="tpu_custom_call" | custom-call | tf_op jit(solution)/shard_map/prefix/pallas_call | solution.py:442
  26.9 15.1 %all-to-all-start.1 = ((f32[128,1,128]{2,1,0:T(1,128)}), f32[128,1,128]{2,1,0:T(1,128)S(1)}, u32[]{:S(2)}, u32[]{:S(2)}) async-start(f32[128,1,128]{2,1,0:T(1,128)} %bitcast.5), calls=%async_computation.1 | async-start | bytes 131072 | tf_op jit(solution)/shard_map/all_to_all | solution.py:450
  42.0 0.0 copy-done
  42.1 2.2 %collective-permute-start.1 = (f32[8,1,1,1280]{3,2,1,0:T(1,128)S(1)}, f32[8,1,1,1280]{3,2,1,0:T(1,128)S(1)}, u32[]{:S(2)}, u32[]{:S(2)}) collective-permute-start(f32[8,1,1,1280]{3,2,1,0:T(1,128)S(1)} %copy-done), channel_id=1, source_target_pairs={{0,1},{2,3},{4,5},{6,7},{8,9},{10,11},{12,13},{14,15},{1,0},{3,2},... | collective-permute-start | bytes 122888 | tf_op jit(solution)/shard_map/ppermute | solution.py:390
  44.3 4.4 %collective-permute-start = (f32[8,1,1,1280]{3,2,1,0:T(1,128)S(1)}, f32[8,1,1,1280]{3,2,1,0:T(1,128)S(1)}, u32[]{:S(2)}, u32[]{:S(2)}) collective-permute-start(f32[8,1,1,1280]{3,2,1,0:T(1,128)S(1)} %copy-done), channel_id=1, source_target_pairs={{1,2},{3,4},{5,6},{7,8},{9,10},{11,12},{13,14},{2,1},{4,3},{6,5},{... | collective-permute-start | bytes 122888 | tf_op jit(solution)/shard_map/ppermute | solution.py:390
  48.6 0.0 copy-done.1
  48.7 0.1 reshape.45.owner_ref
  50.1 0.7 tables.1
  50.7 0.0 collective-permute-done.1
  50.8 4.4 %collective-permute-done = f32[8,1,1,1280]{3,2,1,0:T(1,128)S(1)} collective-permute-done((f32[8,1,1,1280]{3,2,1,0:T(1,128)S(1)}, f32[8,1,1,1280]{3,2,1,0:T(1,128)S(1)}, u32[]{:S(2)}, u32[]{:S(2)}) %collective-permute-start) | collective-permute-done | bytes 40992 | tf_op jit(solution)/shard_map/ppermute | solution.py:390
  55.1 0.0 all-to-all-done.1
  55.1 1.1 %grid.1 = f32[256,128]{1,0:T(8,128)S(1)} custom-call(f32[128,128]{1,0:T(8,128)S(1)} %bitcast.17, bf16[640,256]{1,0:T(8,128)(2,1)S(1)} %get-tuple-element.16.table_high_ref, bf16[640,256]{1,0:T(8,128)(2,1)S(1)} %get-tuple-element.17.table_low_ref, f32[80,128]{1,0:T(8,128)S(1)} %get-tuple-element.18.phase_cos_ref, ...), custom_call_target="tpu_custom_call" | custom-call | tf_op jit(solution)/shard_map/grid/pallas_call | solution.py:459
  56.2 20.9 %all_to_all.16 = f32[64,4,128]{2,1,0:T(4,128)S(1)} all-to-all(f32[64,4,128]{2,1,0:T(4,128)S(1)} %bitcast.16), channel_id=1, replica_groups=mesh['wave'=64,'lev'=16] {'wave'}, dimensions={0} | all-to-all | bytes 262144 | tf_op jit(solution)/shard_map/all_to_all | solution.py:477
  77.1 1.3 %result.1 = f32[800,128]{1,0:T(8,128)} custom-call(f32[256,128]{1,0:T(8,128)S(1)} %bitcast.15, bf16[640,640]{1,0:T(8,128)(2,1)S(1)} %get-tuple-element.21.high_ref, bf16[640,640]{1,0:T(8,128)(2,1)S(1)} %get-tuple-element.22.low_ref), custom_call_target="tpu_custom_call" | custom-call | tf_op jit(solution)/shard_map/result/pallas_call | solution.py:480
Async XLA Ops:
  0.0 48.6 %copy-start.1 = (s32[640]{0:T(1024)S(1)}, s32[640]{0:T(1024)}, u32[]{:S(2)}) copy-start(s32[640]{0:T(1024)} %owner_hbm.1) | copy-start | bytes 7684
  0.0 42.0 %copy-start = (f32[8,1,1,1280]{3,2,1,0:T(1,128)S(1)}, f32[8,1,1,1280]{3,2,1,0:T(1,128)}, u32[]{:S(2)}) copy-start(f32[8,1,1,1280]{3,2,1,0:T(1,128)} %param.13) | copy-start | bytes 122884
  26.9 28.2 %all-to-all-start.1 = ((f32[128,1,128]{2,1,0:T(1,128)}), f32[128,1,128]{2,1,0:T(1,128)S(1)}, u32[]{:S(2)}, u32[]{:S(2)}) async-start(f32[128,1,128]{2,1,0:T(1,128)} %bitcast.5), calls=%async_computation.1 | async-start | bytes 131072 | tf_op jit(solution)/shard_map/all_to_all | solution.py:450
  42.1 8.7 %collective-permute-start.1 = (f32[8,1,1,1280]{3,2,1,0:T(1,128)S(1)}, f32[8,1,1,1280]{3,2,1,0:T(1,128)S(1)}, u32[]{:S(2)}, u32[]{:S(2)}) collective-permute-start(f32[8,1,1,1280]{3,2,1,0:T(1,128)S(1)} %copy-done), channel_id=1, source_target_pairs={{0,1},{2,3},{4,5},{6,7},{8,9},{10,11},{12,13},{14,15},{1,0},{3,2},... | collective-permute-start | bytes 122888 | tf_op jit(solution)/shard_map/ppermute | solution.py:390
  44.3 10.9 %collective-permute-start = (f32[8,1,1,1280]{3,2,1,0:T(1,128)S(1)}, f32[8,1,1,1280]{3,2,1,0:T(1,128)S(1)}, u32[]{:S(2)}, u32[]{:S(2)}) collective-permute-start(f32[8,1,1,1280]{3,2,1,0:T(1,128)S(1)} %copy-done), channel_id=1, source_target_pairs={{1,2},{3,4},{5,6},{7,8},{9,10},{11,12},{13,14},{2,1},{4,3},{6,5},{... | collective-permute-start | bytes 122888 | tf_op jit(solution)/shard_map/ppermute | solution.py:390

commit v6 on v3

--- a/solution.py
+++ b/solution.py
@@ -1,3 +1,4 @@
+import functools
 import math
 
 import jax
@@ -268,9 +269,15 @@
     q_ref,
     above_ref,
     below_ref,
+    far_ref,
     factor_ref,
-    out_ref,
+    *rest,
+    depth,
 ):
+    level_ref, out_ref = rest if INTERPRET else (None, *rest)
+    level = level_ref[0] if INTERPRET else lax.axis_index("lev")
+    first_level = level % depth == 0
+    last_level = level % depth == depth - 1
     waves = got_ref.shape[0] // 2
     pairs = 5
     blocks = phase_cos_ref.shape[0] // pairs
@@ -303,6 +310,9 @@
         q = q_ref[pl.ds(b, 8, stride=used), :]
         above = above_ref[pl.ds(b, 8, stride=used), :]
         below = below_ref[pl.ds(b, 8, stride=used), :]
+        far = far_ref[pl.ds(b, 8, stride=used), :]
+        above = jnp.where(first_level, far, above)
+        below = jnp.where(last_level, far, below)
         field = grid[8 * b : 8 * b + 4, 0:128] + grid[8 * b + 4 : 8 * b + 8, 128:256]
         east.append(field[0:1] * q)
         merid.append(field[1:2] * q)
@@ -380,14 +390,15 @@
     levels = lax.axis_size("lev")
     count, _, _, length = tracers.shape
     call = lambda kernel, **kw: pl.pallas_call(kernel, interpret=INTERPRET, **kw)
-    up = [(i, i + 1) for i in range(levels - 1)]
+    depth = levels // 2
+    up = [(h + z, h + z + 1) for h in (0, depth) for z in range(depth - 1)]
     down = [(b, a) for a, b in up]
+    far = lax.ppermute(tracers, "lev", [(depth - 1, depth), (depth, depth - 1)])
     above = lax.ppermute(tracers, "lev", up)
     below = lax.ppermute(tracers, "lev", down)
     owner = owner_map
     if INTERPRET:
         owner = jnp.concatenate([owner_map, lax.axis_index("wave").reshape(1)])
-    depth = levels // 2
     columns = [[half * depth + z for z in range(depth)] for half in range(2)]
     planes = [
         [w * levels + half * depth + z for half in range(2) for w in range(waves)] for z in range(depth)
@@ -453,9 +464,9 @@
     ).reshape(2 * waves, 128)
     flat = lambda x: local(x.reshape(count * length // 128, 128))
     spectra = call(
-        grid_kernel,
+        functools.partial(grid_kernel, depth=depth),
         name="grid",
-        in_specs=[vmem] * 9,
+        in_specs=[vmem] * 10 + [smem] * len(level),
         out_specs=vmem,
         out_shape=shaped((waves * 4, 128)),
     )(
@@ -467,7 +478,9 @@
         flat(tracers),
         flat(above),
         flat(below),
+        flat(far),
         local(factors),
+        *level,
     )
     back = lax.all_to_all(
         spectra.reshape(waves, 4, 128), "wave", split_axis=0, concat_axis=0, tiled=True

time: 80.6 us -> 78.8 us (0.978)
  waiting for transfers between devices: 6.73 us -> 4.12 us
    ppermute x1, waiting for transfers between devices: 6.72 us -> 0.01 us  [shards(): above = lax.ppermute(tracers, 'lev', up)]
    ppermute x0 -> x1, waiting for transfers between devices: none -> 4.11 us  [shards(): far = lax.ppermute(tracers, 'lev', [(depth - 1, depth), (depth, depth - 1)])]
    ppermute x0 -> x1, starting transfers between devices: none -> 3.33 us  [shards(): far = lax.ppermute(tracers, 'lev', [(depth - 1, depth), (depth, depth - 1)])]
    ppermute x1, starting transfers between devices: 4.23 us -> 1.29 us  [shards(): below = lax.ppermute(tracers, 'lev', down)]
  transfers between devices with their start and end apart: 3 -> 4, of which waited for: 1 -> 1; matrix products, arithmetic and copies ran while one was open for 0% -> 0% of each run, Pallas kernels for 1% -> 1%
where the time goes in v6:
time: 78.8 us; the launch traced here: 78.4 us
  blocking collectives  44.1 us (56%)
  starting transfers between devices  22 us (28%)
  Pallas kernels  6.05 us (8%)
  waiting for transfers between devices  4.12 us (5%)
  between operations  2.07 us (3%)
    all_to_all x1, blocking collectives, shards(): lax.all_to_all(message.reshape(depth, 1, slots * 128), 'lev', split_axis=...  23.2 us
    all_to_all x1, blocking collectives, shards(): lax.all_to_all(spectra.reshape(waves, 4, 128), 'wave', split_axis=0, conc...  20.9 us
    all_to_all x1, starting transfers between devices, shards(): lax.all_to_all(sent.reshape(2 * rows, 1, 128), ('wave', 'lev'), split_axi...  15.1 us
    ppermute x1, waiting for transfers between devices, shards(): far = lax.ppermute(tracers, 'lev', [(depth - 1, depth), (depth, depth - 1)])  4.11 us
    ppermute x1, starting transfers between devices, shards(): far = lax.ppermute(tracers, 'lev', [(depth - 1, depth), (depth, depth - 1)])  3.33 us
    pallas_call x1, Pallas kernels, shards(): call(winds_kernel, name='winds', in_specs=[hbm, hbm, hbm, hbm], out_specs...  2.2 us
    ppermute x1, starting transfers between devices, shards(): above = lax.ppermute(tracers, 'lev', up)  2.19 us
  transfers between devices with their start and end apart: 4, of which 1 were waited for; matrix products, arithmetic and copies ran while one was open for 0% of the time, Pallas kernels for 1%

profile of v6, /device:TPU:113, one launch (start us, length us, event | category | flops | bytes accessed | tf_op | source)
XLA Modules:
  0.0 78.4 jit_solution(18092768276585604954)
XLA Ops:
  0.0 0.0 copy-start.1
  0.0 0.0 copy-start
  0.7 2.2 %winds.1 = (f32[40,128]{1,0:T(8,128)S(1)}, f32[80,128]{1,0:T(8,128)S(1)}, bf16[640,640]{1,0:T(8,128)(2,1)S(1)}, bf16[640,640]{1,0:T(8,128)(2,1)S(1)}) custom-call(f32[200,128]{1,0:T(8,128)} %bitcast.25, f32[10,64,640]{2,1,0:T(8,128)} %leg_hbm.1, s32[640]{0:T(1024)} %owner_hbm.1, f32[1,1]{1,0:T(1,128)} %bitcast.15.thick_hbm), custom_call_target="tpu_custom_call" | custom-call | tf_op jit(solution)/shard_map/winds/pallas_call | solution.py:407
  2.9 23.2 %all_to_all.15 = f32[8,1,1280]{2,1,0:T(1,128)S(1)} all-to-all(f32[8,1,1280]{2,1,0:T(1,128)S(1)} %bitcast.24), channel_id=1, replica_groups={{0,1,2,3,4,5,6,7},{8,9,10,11,12,13,14,15},{16,17,18,19,20,21,22,23},{24..., dimensions={0} | all-to-all | bytes 81920 | tf_op jit(solution)/shard_map/all_to_all | solution.py:428
  26.1 0.8 %prefix.1 = f32[128,128]{1,0:T(8,128)} custom-call(f32[80,128]{1,0:T(8,128)S(1)} %bitcast.19, f32[40,128]{1,0:T(8,128)S(1)} %get-tuple-element.15.f_ref), custom_call_target="tpu_custom_call" | custom-call | tf_op jit(solution)/shard_map/prefix/pallas_call | solution.py:449
  26.9 15.1 %all-to-all-start.1 = ((f32[128,1,128]{2,1,0:T(1,128)}), f32[128,1,128]{2,1,0:T(1,128)S(1)}, u32[]{:S(2)}, u32[]{:S(2)}) async-start(f32[128,1,128]{2,1,0:T(1,128)} %bitcast.5), calls=%async_computation.1 | async-start | bytes 131072 | tf_op jit(solution)/shard_map/all_to_all | solution.py:457
  42.0 0.0 copy-done
  42.1 2.2 %collective-permute-start = (f32[8,1,1,1280]{3,2,1,0:T(1,128)S(1)}, f32[8,1,1,1280]{3,2,1,0:T(1,128)S(1)}, u32[]{:S(2)}, u32[]{:S(2)}) collective-permute-start(f32[8,1,1,1280]{3,2,1,0:T(1,128)S(1)} %copy-done), channel_id=1, source_target_pairs={{0,1},{1,2},{2,3},{3,4},{4,5},{5,6},{6,7},{8,9},{9,10},{10,11},{11... | collective-permute-start | bytes 122888 | tf_op jit(solution)/shard_map/ppermute | solution.py:397
  44.2 3.3 %collective-permute-start.2 = (f32[8,1,1,1280]{3,2,1,0:T(1,128)S(1)}, f32[8,1,1,1280]{3,2,1,0:T(1,128)S(1)}, u32[]{:S(2)}, u32[]{:S(2)}) collective-permute-start(f32[8,1,1,1280]{3,2,1,0:T(1,128)S(1)} %copy-done), channel_id=1, source_target_pairs={{7,8},{8,7},{23,24},{24,23},{39,40},{40,39},{55,56},{56,55},{71,72... | collective-permute-start | bytes 122888 | tf_op jit(solution)/shard_map/ppermute | solution.py:396
  47.6 1.3 %collective-permute-start.1 = (f32[8,1,1,1280]{3,2,1,0:T(1,128)S(1)}, f32[8,1,1,1280]{3,2,1,0:T(1,128)S(1)}, u32[]{:S(2)}, u32[]{:S(2)}) collective-permute-start(f32[8,1,1,1280]{3,2,1,0:T(1,128)S(1)} %copy-done), channel_id=1, source_target_pairs={{1,0},{2,1},{3,2},{4,3},{5,4},{6,5},{7,6},{9,8},{10,9},{11,10},{12... | collective-permute-start | bytes 122888 | tf_op jit(solution)/shard_map/ppermute | solution.py:398
  48.9 0.0 copy-done.1
  48.9 0.1 reshape.48.owner_ref
  50.3 0.7 tables.1
  51.0 0.0 collective-permute-done
  51.0 4.1 %collective-permute-done.2 = f32[8,1,1,1280]{3,2,1,0:T(1,128)S(1)} collective-permute-done((f32[8,1,1,1280]{3,2,1,0:T(1,128)S(1)}, f32[8,1,1,1280]{3,2,1,0:T(1,128)S(1)}, u32[]{:S(2)}, u32[]{:S(2)}) %collective-permute-start.2) | collective-permute-done | bytes 40992 | tf_op jit(solution)/shard_map/ppermute | solution.py:396
  55.1 0.0 collective-permute-done.1
  55.1 0.0 all-to-all-done.1
  55.1 1.1 %grid.1 = f32[256,128]{1,0:T(8,128)S(1)} custom-call(f32[128,128]{1,0:T(8,128)S(1)} %bitcast.18, bf16[640,256]{1,0:T(8,128)(2,1)S(1)} %get-tuple-element.16.table_high_ref, bf16[640,256]{1,0:T(8,128)(2,1)S(1)} %get-tuple-element.17.table_low_ref, f32[80,128]{1,0:T(8,128)S(1)} %get-tuple-element.18.phase_cos_ref, ...), custom_call_target="tpu_custom_call" | custom-call | tf_op jit(solution)/shard_map/grid/pallas_call | solution.py:466
  56.2 20.9 %all_to_all.16 = f32[64,4,128]{2,1,0:T(4,128)S(1)} all-to-all(f32[64,4,128]{2,1,0:T(4,128)S(1)} %bitcast.16), channel_id=1, replica_groups=mesh['wave'=64,'lev'=16] {'wave'}, dimensions={0} | all-to-all | bytes 262144 | tf_op jit(solution)/shard_map/all_to_all | solution.py:485
  77.1 1.3 %result.1 = f32[800,128]{1,0:T(8,128)} custom-call(f32[256,128]{1,0:T(8,128)S(1)} %bitcast.17, bf16[640,640]{1,0:T(8,128)(2,1)S(1)} %get-tuple-element.21.high_ref, bf16[640,640]{1,0:T(8,128)(2,1)S(1)} %get-tuple-element.22.low_ref), custom_call_target="tpu_custom_call" | custom-call | tf_op jit(solution)/shard_map/result/pallas_call | solution.py:488
Async XLA Ops:
  0.0 48.9 %copy-start.1 = (s32[640]{0:T(1024)S(1)}, s32[640]{0:T(1024)}, u32[]{:S(2)}) copy-start(s32[640]{0:T(1024)} %owner_hbm.1) | copy-start | bytes 7684
  0.0 42.0 %copy-start = (f32[8,1,1,1280]{3,2,1,0:T(1,128)S(1)}, f32[8,1,1,1280]{3,2,1,0:T(1,128)}, u32[]{:S(2)}) copy-start(f32[8,1,1,1280]{3,2,1,0:T(1,128)} %param.13) | copy-start | bytes 122884
  26.9 28.2 %all-to-all-start.1 = ((f32[128,1,128]{2,1,0:T(1,128)}), f32[128,1,128]{2,1,0:T(1,128)S(1)}, u32[]{:S(2)}, u32[]{:S(2)}) async-start(f32[128,1,128]{2,1,0:T(1,128)} %bitcast.5), calls=%async_computation.1 | async-start | bytes 131072 | tf_op jit(solution)/shard_map/all_to_all | solution.py:457
  42.1 8.9 %collective-permute-start = (f32[8,1,1,1280]{3,2,1,0:T(1,128)S(1)}, f32[8,1,1,1280]{3,2,1,0:T(1,128)S(1)}, u32[]{:S(2)}, u32[]{:S(2)}) collective-permute-start(f32[8,1,1,1280]{3,2,1,0:T(1,128)S(1)} %copy-done), channel_id=1, source_target_pairs={{0,1},{1,2},{2,3},{3,4},{4,5},{5,6},{6,7},{8,9},{9,10},{10,11},{11... | collective-permute-start | bytes 122888 | tf_op jit(solution)/shard_map/ppermute | solution.py:397
  44.2 10.9 %collective-permute-start.2 = (f32[8,1,1,1280]{3,2,1,0:T(1,128)S(1)}, f32[8,1,1,1280]{3,2,1,0:T(1,128)S(1)}, u32[]{:S(2)}, u32[]{:S(2)}) collective-permute-start(f32[8,1,1,1280]{3,2,1,0:T(1,128)S(1)} %copy-done), channel_id=1, source_target_pairs={{7,8},{8,7},{23,24},{24,23},{39,40},{40,39},{55,56},{56,55},{71,72... | collective-permute-start | bytes 122888 | tf_op jit(solution)/shard_map/ppermute | solution.py:396
  47.6 7.5 %collective-permute-start.1 = (f32[8,1,1,1280]{3,2,1,0:T(1,128)S(1)}, f32[8,1,1,1280]{3,2,1,0:T(1,128)S(1)}, u32[]{:S(2)}, u32[]{:S(2)}) collective-permute-start(f32[8,1,1,1280]{3,2,1,0:T(1,128)S(1)} %copy-done), channel_id=1, source_target_pairs={{1,0},{2,1},{3,2},{4,3},{5,4},{6,5},{7,6},{9,8},{10,9},{11,10},{12... | collective-permute-start | bytes 122888 | tf_op jit(solution)/shard_map/ppermute | solution.py:398
